TPU v7x, 32 devices: a whole 2x2x4 slice. The times are simulated.
32 devices in a mesh: sec: 4 (over y, x), ctx: 8 (over z, core).
Axes of the slice: x: 2, y: 2, z: 4, core: 2. Of those that a mesh axis runs over, the one named last changes fastest.
Arguments:
- hidden_state: bfloat16 [4, 1024, 4096], P('sec', 'ctx'), may hold values from -8 to 8
- queries: bfloat16 [4, 1024, 4096], P('sec', 'ctx'), may hold values from -6 to 6
- key_vectors: bfloat16 [4, 1024, 4096], P('sec', 'ctx'), may hold values from -4.5 to 4.5
- value_vectors: bfloat16 [4, 1024, 4096], P('sec', 'ctx'), may hold values from -6 to 6
- modulation: float32 [32, 3, 4096], replicated, may hold values from -3 to 3
- down_weight: bfloat16 [4096, 256], replicated, may hold values from -0.09375 to 0.09375
- conv_weight: bfloat16 [3, 3, 3, 256, 256], replicated, may hold values from -0.078125 to 0.078125
- clip_frames: int32 [4], replicated, may hold values from 4 to 16, as said below
- destination: int32 [4], replicated, may hold values from 0 to 3, as said below
- timestep: int32 [4], replicated, may hold values from 0 to 31
Outputs:
- upsampled: bfloat16 [4, 1024, 256], P('sec', 'ctx')
Inputs may be any that keep to these rules, and one draw needn't show every extreme that they name: `clip_frames`: one section's clip fills all 16 frames. `destination`: every upsampler group receives exactly one clip; some group d receives the clip of section (d + 2) mod 4.
All inputs are finite; a program needn't handle non-finite values.
Results may differ from a plain program's by a relative error of at most 0.0063.
Values may be sent and summed in bfloat16 or wider, within the bound.
No kernel may reach another device: no remote copies, remote signals or barrier semaphores. Data moves between devices by JAX's collectives and lax.ppermute only.
A program may use at most 64 MiB of HBM per device.

v0:
```python
import functools
import itertools
import math

import jax
import jax.numpy as jnp
from jax import lax
from jax.experimental import pallas as pl
from jax.experimental.pallas import tpu as pltpu
from jax.sharding import PartitionSpec as P


HEADS = 32
HH = 8
WW = 8


def head_chunks(count):
    local_heads = HEADS // count
    return (local_heads - 1, 1) if local_heads > 1 else (1,)


def partner(me, step, count):
    if count & (count - 1) == 0:
        return me ^ step, me ^ step
    return lax.rem(me + step, count), lax.rem(me - step + count, count)


def ring(step, count):
    if count & (count - 1) == 0:
        return [(i, i ^ step) for i in range(count)]
    return [(i, (i + step) % count) for i in range(count)]


def exchange(pieces, axis, count):
    out = [pieces[0]] + [None] * (count - 1)
    for step in range(1, count):
        out[step] = lax.ppermute(pieces[step], axis, ring(step, count))
    return out


def pack_kernel(count, kinds, head_cols, first_col, width, *rest):
    sources, outs, (buf, in_sem, out_sem) = rest[:kinds], rest[kinds : kinds + count], rest[kinds + count :]
    me = lax.axis_index("ctx")
    order = list(range(count - 1, -1, -1))

    def load(step, kind):
        col = pl.multiple_of(partner(me, step, count)[0] * head_cols + first_col, 128)
        return pltpu.make_async_copy(
            sources[kind].at[0, :, pl.ds(col, width)], buf.at[step, kind], in_sem.at[step, kind]
        )

    def save(step):
        return pltpu.make_async_copy(buf.at[step], outs[step], out_sem.at[step])

    for step in order:
        for kind in range(kinds):
            load(step, kind).start()
    for step in order:
        for kind in range(kinds):
            load(step, kind).wait()
        save(step).start()
    for step in order:
        save(step).wait()


def pack(sources, count, head_cols, first_col, width):
    rows = sources[0].shape[1]
    kinds = len(sources)
    piece = jax.ShapeDtypeStruct((kinds, rows, width), sources[0].dtype)
    return pl.pallas_call(
        functools.partial(pack_kernel, count, kinds, head_cols, first_col, width),
        out_shape=[piece] * count,
        in_specs=[pl.BlockSpec(memory_space=pltpu.HBM)] * kinds,
        out_specs=[pl.BlockSpec(memory_space=pltpu.HBM)] * count,
        scratch_shapes=[
            pltpu.VMEM((count, kinds, rows, width), sources[0].dtype),
            pltpu.SemaphoreType.DMA((count, kinds)),
            pltpu.SemaphoreType.DMA((count,)),
        ],
        cost_estimate=pl.CostEstimate(
            flops=0, bytes_accessed=4 * kinds * count * rows * width, transcendentals=0
        ),
        name="pack",
    )(*sources)


def attend_kernel(count, heads, block_rows, frames_ref, *rest):
    pieces, outs = rest[:count], rest[count : 2 * count]
    data, values, result, in_sem, value_sem, out_sem = rest[2 * count :]
    me = lax.axis_index("ctx")
    rows = pieces[0].shape[1]
    seq = count * rows
    size = pieces[0].shape[2] // heads
    scale = math.log2(math.e) / math.sqrt(size)

    def place(step):
        return pl.ds(pl.multiple_of(partner(me, step, count)[1] * rows, rows), rows)

    def load(step):
        return pltpu.make_async_copy(
            pieces[step].at[pl.ds(0, 2)], data.at[:, place(step), :], in_sem.at[step]
        )

    def load_values(step, head):
        return pltpu.make_async_copy(
            pieces[step].at[2, :, pl.ds(head * size, size)],
            values.at[place(step), pl.ds(head * 2 * size, size)],
            value_sem.at[head, step],
        )

    def save(step):
        return pltpu.make_async_copy(result.at[place(step), :], outs[step], out_sem.at[step])

    for step in range(count):
        load(step).start()
    for head in range(heads):
        for step in range(count):
            load_values(step, head).start()
    for head in range(heads):
        values[:, pl.ds((head * 2 + 1) * size, size)] = jnp.ones((seq, size), jnp.bfloat16)
    for step in range(count):
        load(step).wait()
    for head in range(heads):
        for step in range(count):
            load_values(step, head).wait()
    valid = frames_ref[0] * (HH * WW)
    places = lax.broadcasted_iota(jnp.int32, (1, seq), 1)
    bias = jnp.where(places < valid, 0.0, -jnp.inf)

    def block(index, carry):
        start = pl.multiple_of(index * block_rows, block_rows)
        here = pl.ds(start, block_rows)
        for head in range(heads):
            lanes = pl.ds(head * size, size)
            scores = lax.dot_general(
                data[0, here, lanes],
                data[1, :, lanes],
                (((1,), (1,)), ((), ())),
                preferred_element_type=jnp.float32,
            )
            scores = scores * scale + bias
            weights = jnp.exp2(scores - jnp.max(scores, axis=1, keepdims=True))
            both = jnp.dot(
                weights.astype(jnp.bfloat16),
                values[:, pl.ds(head * 2 * size, 2 * size)],
                preferred_element_type=jnp.float32,
            )
            result[here, lanes] = (both[:, :size] / both[:, size:]).astype(result.dtype)
        return carry

    lax.fori_loop(0, seq // block_rows, block, 0)
    for step in range(count):
        save(step).start()
    for step in range(count):
        save(step).wait()


def attend(frames, pieces, count, heads):
    _, rows, width = pieces[0].shape
    seq = count * rows
    block_rows = min(256, seq)
    return pl.pallas_call(
        functools.partial(attend_kernel, count, heads, block_rows),
        out_shape=[jax.ShapeDtypeStruct((rows, width), jnp.bfloat16)] * count,
        in_specs=[pl.BlockSpec(memory_space=pltpu.SMEM)]
        + [pl.BlockSpec(memory_space=pltpu.HBM)] * count,
        out_specs=[pl.BlockSpec(memory_space=pltpu.HBM)] * count,
        scratch_shapes=[
            pltpu.VMEM((2, seq, width), jnp.bfloat16),
            pltpu.VMEM((seq, 2 * width), jnp.bfloat16),
            pltpu.VMEM((seq, width), jnp.bfloat16),
            pltpu.SemaphoreType.DMA((count,)),
            pltpu.SemaphoreType.DMA((heads, count)),
            pltpu.SemaphoreType.DMA((count,)),
        ],
        cost_estimate=pl.CostEstimate(
            flops=6 * seq * seq * width,
            bytes_accessed=8 * seq * width,
            transcendentals=seq * seq * heads,
        ),
        name="attend",
    )(frames, *pieces)


def project_kernel(count, frames_ref, h_ref, mod_ref, weight_ref, *rest):
    pieces, rest = rest[:count], rest[count:]
    out_ref, attended, hidden, weight, mod_rows, in_sem, mod_sem, h_sem, weight_sem = rest
    me = lax.axis_index("ctx")
    rows, width = pieces[0].shape
    block_rows = 16

    def load(step):
        owner = partner(me, step, count)[1]
        col = pl.multiple_of(owner * width, 128)
        return pltpu.make_async_copy(
            pieces[step], attended.at[:, pl.ds(col, width)], in_sem.at[step]
        )

    mod_copy = pltpu.make_async_copy(mod_ref, mod_rows, mod_sem)
    h_copy = pltpu.make_async_copy(h_ref.at[0], hidden, h_sem)
    weight_copy = pltpu.make_async_copy(weight_ref, weight, weight_sem)
    mod_copy.start()
    h_copy.start()
    for step in range(count):
        load(step).start()
    weight_copy.start()
    mod_copy.wait()
    h_copy.wait()
    for step in range(count):
        load(step).wait()

    def rows_of(index, carry):
        here = pl.ds(pl.multiple_of(index * block_rows, block_rows), block_rows)
        block = (
            hidden[here, :].astype(jnp.float32)
            + mod_rows[2:3, :] * attended[here, :].astype(jnp.float32)
        ).astype(jnp.bfloat16)
        wide = block.astype(jnp.float32)
        centre = jnp.mean(wide, axis=-1, keepdims=True)
        spread = jnp.mean(jnp.square(wide - centre), axis=-1, keepdims=True)
        normed = (wide - centre) * lax.rsqrt(spread + 1e-06) * (
            1.0 + mod_rows[1:2, :]
        ) + mod_rows[0:1, :]
        attended[here, :] = normed.astype(jnp.bfloat16)
        return carry

    lax.fori_loop(0, rows // block_rows, rows_of, 0)
    weight_copy.wait()
    projected = jnp.dot(attended[...], weight[...], preferred_element_type=jnp.float32)
    token = me * rows + lax.broadcasted_iota(jnp.int32, (rows, 1), 0)
    out_ref[...] = jnp.where(token < frames_ref[0] * (HH * WW), projected, 0.0).astype(
        out_ref.dtype
    )


def project(frames, hidden_state, modulation, down_weight, pieces, count):
    _, rows, model = hidden_state.shape
    channels = down_weight.shape[1]
    return pl.pallas_call(
        functools.partial(project_kernel, count),
        out_shape=jax.ShapeDtypeStruct((rows, channels), jnp.bfloat16),
        in_specs=[pl.BlockSpec(memory_space=pltpu.SMEM)]
        + [pl.BlockSpec(memory_space=pltpu.HBM)] * (count + 3),
        out_specs=pl.BlockSpec(memory_space=pltpu.VMEM),
        scratch_shapes=[
            pltpu.VMEM((rows, model), jnp.bfloat16),
            pltpu.VMEM((rows, model), jnp.bfloat16),
            pltpu.VMEM((model, channels), jnp.bfloat16),
            pltpu.VMEM((3, model), jnp.float32),
            pltpu.SemaphoreType.DMA((count,)),
            pltpu.SemaphoreType.DMA,
            pltpu.SemaphoreType.DMA,
            pltpu.SemaphoreType.DMA,
        ],
        cost_estimate=pl.CostEstimate(
            flops=2 * rows * model * channels,
            bytes_accessed=4 * rows * model + 2 * model * channels,
            transcendentals=0,
        ),
        name="project",
    )(frames, hidden_state, modulation, down_weight, *pieces)


def constants_kernel(mod_ref, weight_ref, out_ref):
    def product(row):
        high = row.astype(jnp.bfloat16)
        low = (row - high.astype(jnp.float32)).astype(jnp.bfloat16)
        split = jnp.concatenate(
            [jnp.broadcast_to(high, (8,) + high.shape[1:]), jnp.broadcast_to(low, (8,) + low.shape[1:])],
            axis=0,
        )
        both = jnp.dot(split, weight_ref[...], preferred_element_type=jnp.float32)
        return both[:8] + both[8:]

    out_ref[0] = product(1.0 + mod_ref[1:2, :])
    out_ref[1] = product(mod_ref[0:1, :])


def constants(mod_rows, down_weight):
    model, channels = down_weight.shape
    return pl.pallas_call(
        constants_kernel,
        out_shape=jax.ShapeDtypeStruct((2, 8, channels), jnp.float32),
        in_specs=[pl.BlockSpec(memory_space=pltpu.VMEM)] * 2,
        out_specs=pl.BlockSpec(memory_space=pltpu.VMEM),
        cost_estimate=pl.CostEstimate(
            flops=64 * model * channels, bytes_accessed=2 * model * channels, transcendentals=0
        ),
        name="constants",
    )(mod_rows, down_weight)


def early_kernel(count, head_cols, h_ref, mod_ref, weight_ref, *rest):
    pieces, rest = rest[:count], rest[count:]
    acc_ref, centre_ref, square_ref, late_h, late_mod, late_weight = rest[:6]
    attended, hidden, weight, mod, in_sem, h_sem, mod_sem, weight_sem, late_sem = rest[6:]
    me = lax.axis_index("ctx")
    rows, width = pieces[0].shape
    late = head_cols - width
    block_rows = 16

    def copies(step):
        col = pl.multiple_of(partner(me, step, count)[1] * head_cols, 128)
        here = pl.ds(step * width, width)
        return (
            pltpu.make_async_copy(pieces[step], attended.at[:, here], in_sem.at[step]),
            pltpu.make_async_copy(
                h_ref.at[0, :, pl.ds(col, width)], hidden.at[:, here], h_sem.at[step]
            ),
            pltpu.make_async_copy(
                mod_ref.at[:, pl.ds(col, width)], mod.at[:, here], mod_sem.at[step]
            ),
            pltpu.make_async_copy(
                weight_ref.at[pl.ds(col, width), :], weight.at[here, :], weight_sem.at[step]
            ),
        )

    def late_copies(step):
        col = pl.multiple_of(partner(me, step, count)[1] * head_cols + width, 128)
        here = pl.ds(step * late, late)
        return (
            pltpu.make_async_copy(
                h_ref.at[0, :, pl.ds(col, late)], late_h.at[:, here], late_sem.at[0, step]
            ),
            pltpu.make_async_copy(
                mod_ref.at[:, pl.ds(col, late)], late_mod.at[:, here], late_sem.at[1, step]
            ),
            pltpu.make_async_copy(
                weight_ref.at[pl.ds(col, late), :], late_weight.at[here, :], late_sem.at[2, step]
            ),
        )

    for step in range(count):
        for copy in copies(step):
            copy.start()
    for step in range(count):
        for copy in late_copies(step):
            copy.start()
    for step in range(count):
        for copy in copies(step)[:3]:
            copy.wait()

    def rows_of(index, carry):
        here = pl.ds(pl.multiple_of(index * block_rows, block_rows), block_rows)
        wide = (
            (
                hidden[here, :].astype(jnp.float32)
                + mod[2:3, :] * attended[here, :].astype(jnp.float32)
            )
            .astype(jnp.bfloat16)
            .astype(jnp.float32)
        )
        centre = jnp.mean(wide, axis=-1, keepdims=True)
        away = wide - centre
        square = jnp.sum(jnp.square(away), axis=-1, keepdims=True)
        attended[here, :] = (away * (1.0 + mod[1:2, :])).astype(jnp.bfloat16)
        centre_ref[here, :] = jnp.broadcast_to(centre, (block_rows, 128))
        square_ref[here, :] = jnp.broadcast_to(square, (block_rows, 128))
        return carry

    lax.fori_loop(0, rows // block_rows, rows_of, 0)
    for step in range(count):
        copies(step)[3].wait()
    acc_ref[...] = jnp.dot(attended[...], weight[...], preferred_element_type=jnp.float32)
    for step in range(count):
        for copy in late_copies(step):
            copy.wait()


def project_early(hidden_state, mod_rows, down_weight, pieces, count):
    _, rows, model = hidden_state.shape
    channels = down_weight.shape[1]
    head_cols = model // count
    width = pieces[0].shape[1]
    late = head_cols - width
    hbm = pl.BlockSpec(memory_space=pltpu.HBM)
    vmem = pl.BlockSpec(memory_space=pltpu.VMEM)
    return pl.pallas_call(
        functools.partial(early_kernel, count, head_cols),
        out_shape=[
            jax.ShapeDtypeStruct((rows, channels), jnp.float32),
            jax.ShapeDtypeStruct((rows, 128), jnp.float32),
            jax.ShapeDtypeStruct((rows, 128), jnp.float32),
            jax.ShapeDtypeStruct((rows, count * late), jnp.bfloat16),
            jax.ShapeDtypeStruct((3, count * late), jnp.float32),
            jax.ShapeDtypeStruct((count * late, channels), jnp.bfloat16),
        ],
        in_specs=[hbm] * (count + 3),
        out_specs=[vmem] * 6,
        scratch_shapes=[
            pltpu.VMEM((rows, count * width), jnp.bfloat16),
            pltpu.VMEM((rows, count * width), jnp.bfloat16),
            pltpu.VMEM((count * width, channels), jnp.bfloat16),
            pltpu.VMEM((3, count * width), jnp.float32),
            pltpu.SemaphoreType.DMA((count,)),
            pltpu.SemaphoreType.DMA((count,)),
            pltpu.SemaphoreType.DMA((count,)),
            pltpu.SemaphoreType.DMA((count,)),
            pltpu.SemaphoreType.DMA((3, count)),
        ],
        cost_estimate=pl.CostEstimate(
            flops=2 * rows * count * width * channels,
            bytes_accessed=4 * rows * model + 2 * model * channels,
            transcendentals=0,
        ),
        name="project_early",
    )(hidden_state, mod_rows, down_weight, *pieces)


def late_kernel(
    count, early, frames_ref, acc_ref, centre_ref, square_ref, h_ref, mod_ref, weight_ref, const_ref, *rest
):
    pieces, (out_ref, attended, in_sem) = rest[:count], rest[count:]
    rows, width = pieces[0].shape
    late = count * width
    model = early + late

    def load(step):
        return pltpu.make_async_copy(
            pieces[step], attended.at[:, pl.ds(step * width, width)], in_sem.at[step]
        )

    for step in range(count):
        load(step).start()
    for step in range(count):
        load(step).wait()
    wide = (
        (h_ref[...].astype(jnp.float32) + mod_ref[2:3, :] * attended[...].astype(jnp.float32))
        .astype(jnp.bfloat16)
        .astype(jnp.float32)
    )
    first = centre_ref[:, :1]
    own = jnp.mean(wide, axis=-1, keepdims=True)
    square = jnp.sum(jnp.square(wide - own), axis=-1, keepdims=True)
    gap = own - first
    centre = first + gap * (late / model)
    spread = (square_ref[:, :1] + square + gap * gap * (early * late / model)) / model
    scaled = ((wide - first) * (1.0 + mod_ref[1:2, :])).astype(jnp.bfloat16)
    total = acc_ref[...] + jnp.dot(scaled, weight_ref[...], preferred_element_type=jnp.float32)
    total = total + (first - centre) * const_ref[0, :1, :]
    total = total * lax.rsqrt(spread + 1e-06) + const_ref[1, :1, :]
    token = lax.axis_index("ctx") * rows + lax.broadcasted_iota(jnp.int32, (rows, 1), 0)
    out_ref[...] = jnp.where(token < frames_ref[0] * (HH * WW), total, 0.0).astype(out_ref.dtype)


def project_late(frames, early, consts, pieces, count, model):
    rows, width = pieces[0].shape
    channels = consts.shape[-1]
    hbm = pl.BlockSpec(memory_space=pltpu.HBM)
    vmem = pl.BlockSpec(memory_space=pltpu.VMEM)
    return pl.pallas_call(
        functools.partial(late_kernel, count, model - count * width),
        out_shape=jax.ShapeDtypeStruct((rows, channels), jnp.bfloat16),
        in_specs=[pl.BlockSpec(memory_space=pltpu.SMEM)] + [vmem] * 7 + [hbm] * count,
        out_specs=vmem,
        scratch_shapes=[
            pltpu.VMEM((rows, count * width), jnp.bfloat16),
            pltpu.SemaphoreType.DMA((count,)),
        ],
        cost_estimate=pl.CostEstimate(
            flops=2 * rows * count * width * channels,
            bytes_accessed=4 * rows * count * width,
            transcendentals=0,
        ),
        name="project_late",
    )(frames, *early, consts, *pieces)


def shifted_frames(frames, channels):
    cells = HH * WW
    column = lax.broadcasted_iota(jnp.int32, (cells, 1), 0) % WW
    blank = jnp.zeros((WW, channels), jnp.float32)
    shifted = []
    for offset in (-1, 0, 1):
        moved = []
        for frame in frames:
            cell = frame.astype(jnp.float32)
            if offset:
                cell = pltpu.roll(cell, (-offset) % cells, 0)
                inside = (column + offset >= 0) & (column + offset < WW)
                cell = jnp.where(inside, cell, 0.0)
            moved.append(jnp.concatenate([blank, cell, blank], axis=0))
        shifted.append(moved)
    return shifted


def window(shifted, across, down):
    cells = HH * WW
    return [f[down * WW : down * WW + cells].astype(jnp.bfloat16) for f in shifted[across]]


def inner_kernel(mid_ref, weight_ref, out_ref, weight, sem):
    cells = HH * WW
    rows, channels = mid_ref.shape
    copy = pltpu.make_async_copy(weight_ref, weight, sem)
    copy.start()
    frames = [mid_ref[pl.ds(start, cells), :] for start in range(0, rows, cells)]
    shifted = shifted_frames(frames, channels)
    copy.wait()
    totals = [frame.astype(jnp.float32) for frame in frames]
    centre = jnp.zeros((rows, channels), jnp.float32)
    for down in range(3):
        for across in range(3):
            picked = window(shifted, across, down)
            centre += jnp.dot(
                jnp.concatenate(picked, axis=0),
                weight[(3 + down) * 3 + across],
                preferred_element_type=jnp.float32,
            )
            for target in range(len(frames)):
                for ahead in (0, 2):
                    if 0 <= target + ahead - 1 < len(frames):
                        totals[target] += jnp.dot(
                            picked[target + ahead - 1],
                            weight[(ahead * 3 + down) * 3 + across],
                            preferred_element_type=jnp.float32,
                        )
    for target in range(len(frames)):
        here = pl.ds(target * cells, cells)
        out_ref[here, :] = totals[target] + centre[target * cells : (target + 1) * cells]


def edge_kernel(frames_ref, inner_ref, even_ref, odd_ref, weight_ref, out_ref, weight, sem):
    cells = HH * WW
    rows, channels = inner_ref.shape
    me = lax.axis_index("ctx")

    def fetch(ahead):
        return pltpu.make_async_copy(
            weight_ref.at[pl.ds(ahead * 9, 9)], weight.at[ahead // 2], sem.at[ahead // 2]
        )

    fetch(0).start()
    fetch(2).start()
    odd = lax.rem(me, 2) == 1
    low = jnp.where(odd, even_ref[...], odd_ref[...])
    high = jnp.where(odd, odd_ref[...], even_ref[...])
    shifted = shifted_frames([low, high], channels)
    first = inner_ref[pl.ds(0, cells), :]
    last = jnp.zeros((cells, channels), jnp.float32)
    fetch(0).wait()
    fetch(2).wait()
    for down in range(3):
        for across in range(3):
            below, above = window(shifted, across, down)
            first += jnp.dot(
                below, weight[0, down * 3 + across], preferred_element_type=jnp.float32
            )
            last += jnp.dot(
                above, weight[1, down * 3 + across], preferred_element_type=jnp.float32
            )
    blank = jnp.zeros((rows - cells, channels), jnp.float32)
    total = jnp.concatenate([first, inner_ref[pl.ds(cells, rows - cells), :]], axis=0)
    total = total + jnp.concatenate([blank, last], axis=0)
    token = me * rows + lax.broadcasted_iota(jnp.int32, (rows, 1), 0)
    out_ref[0] = jnp.where(token < frames_ref[0] * cells, total, 0.0).astype(out_ref.dtype)


def refine(frames, mid, even, odd, conv_weight):
    rows, channels = mid.shape
    taps = conv_weight.reshape(-1, channels, channels)
    hbm = pl.BlockSpec(memory_space=pltpu.HBM)
    vmem = pl.BlockSpec(memory_space=pltpu.VMEM)
    inner = pl.pallas_call(
        inner_kernel,
        out_shape=jax.ShapeDtypeStruct((rows, channels), jnp.float32),
        in_specs=[vmem, hbm],
        out_specs=vmem,
        scratch_shapes=[pltpu.VMEM(taps.shape, taps.dtype), pltpu.SemaphoreType.DMA],
        cost_estimate=pl.CostEstimate(
            flops=36 * rows * channels * channels,
            bytes_accessed=2 * taps.size + 6 * rows * channels,
            transcendentals=0,
        ),
        name="refine_inner",
    )(mid, taps)
    return pl.pallas_call(
        edge_kernel,
        out_shape=jax.ShapeDtypeStruct((1, rows, channels), jnp.bfloat16),
        in_specs=[pl.BlockSpec(memory_space=pltpu.SMEM)] + [vmem] * 3 + [hbm],
        out_specs=vmem,
        scratch_shapes=[
            pltpu.VMEM((2, 9) + taps.shape[1:], taps.dtype),
            pltpu.SemaphoreType.DMA((2,)),
        ],
        cost_estimate=pl.CostEstimate(
            flops=18 * rows * channels * channels,
            bytes_accessed=2 * taps.size + 6 * rows * channels,
            transcendentals=0,
        ),
        name="refine_edge",
    )(frames, inner, even, odd, taps)


def handoff(projected, destination, source, sec_count):
    if sec_count <= 4:
        orders = [
            order
            for order in itertools.permutations(range(sec_count))
            if any(order[(d + sec_count // 2) % sec_count] == d for d in range(sec_count))
        ]

        def take(order):
            return lambda value: lax.ppermute(value, "sec", list(enumerate(order)))

        codes = jnp.asarray(
            [sum(d * sec_count**i for i, d in enumerate(order)) for order in orders], jnp.int32
        )
        code = jnp.sum(destination * jnp.asarray([sec_count**i for i in range(sec_count)], jnp.int32))
        which = jnp.sum(jnp.where(codes == code, jnp.arange(len(orders), dtype=jnp.int32), 0))
        return lax.switch(which, [take(order) for order in orders], projected)
    my_section = lax.axis_index("sec")
    everyone = exchange([projected] * sec_count, "sec", sec_count)
    chosen = everyone[0]
    for step in range(1, sec_count):
        chosen = jnp.where(
            source == partner(my_section, step, sec_count)[1], everyone[step], chosen
        )
    return chosen


def halos(mid, count):
    cells = HH * WW
    rows, channels = mid.shape
    odd = lax.rem(lax.axis_index("ctx"), 2)
    start = jnp.where(odd == 1, 0, rows - cells)
    inner = [(i, i ^ 1) for i in range(count) if i ^ 1 < count]
    outer = [(i, i + 1) for i in range(1, count - 1, 2)] + [(i + 1, i) for i in range(1, count - 1, 2)]
    crossing = lax.dynamic_slice(mid, (rows - cells - start, 0), (cells, channels))
    beside = lax.dynamic_slice(mid, (start, 0), (cells, channels))
    return lax.ppermute(beside, "ctx", inner), lax.ppermute(crossing, "ctx", outer)


def body(
    hidden_state,
    queries,
    key_vectors,
    value_vectors,
    modulation,
    down_weight,
    conv_weight,
    clip_frames,
    destination,
    timestep,
):
    my_section = lax.axis_index("sec")
    sec_count = lax.axis_size("sec")
    count = lax.axis_size("ctx")
    model_width = hidden_state.shape[2]
    local_heads = HEADS // count
    head_size = model_width // HEADS
    head_cols = local_heads * head_size
    chunks = head_chunks(count)
    section_ids = jnp.arange(destination.shape[0], dtype=jnp.int32)
    source = jnp.sum(jnp.where(destination == my_section, section_ids, 0))
    own_frames = lax.dynamic_slice(clip_frames, (my_section,), (1,))
    clip_length = lax.dynamic_slice(clip_frames, (source,), (1,))
    my_step = timestep[my_section]
    mod_rows = lax.dynamic_index_in_dim(modulation, my_step, 0, keepdims=False)

    received = []
    first_head = 0
    for heads in chunks:
        sent = pack(
            (queries, key_vectors, value_vectors),
            count,
            head_cols,
            first_head * head_size,
            heads * head_size,
        )
        received.append(exchange(sent, "ctx", count))
        first_head += heads
    returned = []
    for chunk, heads in enumerate(chunks):
        outs = attend(own_frames, received[chunk], count, heads)
        returned.append(exchange(outs, "ctx", count))
    if len(chunks) == 1:
        projected = project(
            own_frames, hidden_state, mod_rows, down_weight, returned[0], count
        )
    else:
        early = project_early(hidden_state, mod_rows, down_weight, returned[0], count)
        consts = constants(mod_rows, down_weight)
        projected = project_late(own_frames, early, consts, returned[1], count, model_width)
    mid = handoff(projected, destination, source, sec_count)
    even, odd = halos(mid, count)
    return refine(clip_length, mid, even, odd, conv_weight)


def solution(mesh):
    split = P("sec", "ctx", None)
    return jax.shard_map(
        body,
        mesh=mesh,
        in_specs=(split,) * 4 + (P(),) * 6,
        out_specs=split,
        check_vma=False,
    )
```

profile of v0, /device:TPU:5, one launch (start us, length us, event | category | flops | bytes accessed | tf_op | source)
XLA Modules:
  0.0 156.4 jit_solution(12807586203696279235)
XLA Ops:
  0.0 2.9 %pack.2 = (bf16[3,128,384]{2,1,0:T(8,128)(2,1)}, bf16[3,128,384]{2,1,0:T(8,128)(2,1)}, bf16[3,128,384]{2,1,0:T(8,128)(2,1)}, bf16[3,128,384]{2,1,0:T(8,128)(2,1)...) custom-call(bf16[1,128,4096]{2,1,0:T(8,128)(2,1)} %rest_0_.3, ...), custom_call_target="tpu_custom_call" | custom-call | bytes 4718592 | tf_op jit(solution)/shard_map/pack/pallas_call | solution.py:71
  3.7 1.3 collective-permute-start.16
  5.0 2.0 %pack.3 = (bf16[3,128,128]{2,1,0:T(8,128)(2,1)}, bf16[3,128,128]{2,1,0:T(8,128)(2,1)}, bf16[3,128,128]{2,1,0:T(8,128)(2,1)}, bf16[3,128,128]{2,1,0:T(8,128)(2,1)...) custom-call(bf16[1,128,4096]{2,1,0:T(8,128)(2,1)} %rest_0_.3, ...), custom_call_target="tpu_custom_call" | custom-call | bytes 1572864 | tf_op jit(solution)/shard_map/pack/pallas_call | solution.py:71
  7.6 1.6 %collective-permute-start.17 = (bf16[3,128,384]{2,1,0:T(8,128)(2,1)}, bf16[3,128,384]{2,1,0:T(8,128)(2,1)S(1)}, u32[]{:S(2)}, u32[]{:S(2)}) collective-permute-start(bf16[3,128,384]{2,1,0:T(8,128)(2,1)} %get-tuple-element.77), channel_id=1, source_target_pairs={{0,3},{1,2},{2,1},{3,0},{4,7},{5,6},{6,5},{7,4},{8,11},{9,10},{10,... | collective-permute-start | bytes 884744 | tf_op jit(solution)/shard_map/ppermute | solution.py:38
  9.2 2.3 %collective-permute-start.18 = (bf16[3,128,384]{2,1,0:T(8,128)(2,1)}, bf16[3,128,384]{2,1,0:T(8,128)(2,1)}, u32[]{:S(2)}, u32[]{:S(2)}) collective-permute-start(bf16[3,128,384]{2,1,0:T(8,128)(2,1)} %get-tuple-element.78), channel_id=1, source_target_pairs={{0,4},{1,5},{2,6},{3,7},{4,0},{5,1},{6,2},{7,3},{8,12},{9,13},{10,... | collective-permute-start | bytes 884744 | tf_op jit(solution)/shard_map/ppermute | solution.py:38
  11.5 9.3 %collective-permute-done.30.rest_2_ = bf16[3,128,128]{2,1,0:T(8,128)(2,1)S(1)} collective-permute-done((bf16[3,128,128]{2,1,0:T(8,128)(2,1)}, bf16[3,128,128]{2,1,0:T(8,128)(2,1)S(1)}, u32[]{:S(2)}, u32[]{:S(2)}) %collective-permute-start.30) | collective-permute-done | bytes 98336 | tf_op jit(solution)/shard_map/ppermute | solution.py:38
  20.8 2.9 %collective-permute-start.19 = (bf16[3,128,384]{2,1,0:T(8,128)(2,1)S(1)}, bf16[3,128,384]{2,1,0:T(8,128)(2,1)}, u32[]{:S(2)}, u32[]{:S(2)}) collective-permute-start(bf16[3,128,384]{2,1,0:T(8,128)(2,1)S(1)} %copy-done.25), channel_id=1, source_target_pairs={{0,5},{1,4},{2,7},{3,6},{4,1},{5,0},{6,3},{7,2},{8,13},{9,12},{10,... | collective-permute-start | bytes 884744 | tf_op jit(solution)/shard_map/ppermute | solution.py:38
  24.2 2.0 %collective-permute-start.21 = (bf16[3,128,384]{2,1,0:T(8,128)(2,1)S(1)}, bf16[3,128,384]{2,1,0:T(8,128)(2,1)}, u32[]{:S(2)}, u32[]{:S(2)}) collective-permute-start(bf16[3,128,384]{2,1,0:T(8,128)(2,1)S(1)} %copy-done.22), channel_id=1, source_target_pairs={{0,7},{1,6},{2,5},{3,4},{4,3},{5,2},{6,1},{7,0},{8,15},{9,14},{10,... | collective-permute-start | bytes 884744 | tf_op jit(solution)/shard_map/ppermute | solution.py:38
  29.5 1.4 collective-permute-start.31
  31.4 25.7 %collective-permute-done.19.rest_5_ = bf16[3,128,384]{2,1,0:T(8,128)(2,1)} collective-permute-done((bf16[3,128,384]{2,1,0:T(8,128)(2,1)S(1)}, bf16[3,128,384]{2,1,0:T(8,128)(2,1)}, u32[]{:S(2)}, u32[]{:S(2)}) %collective-permute-start.19) | collective-permute-done | bytes 294944 | tf_op jit(solution)/shard_map/ppermute | solution.py:38
  58.2 2.9 %collective-permute-start.35 = (bf16[3,128,128]{2,1,0:T(8,128)(2,1)}, bf16[3,128,128]{2,1,0:T(8,128)(2,1)S(1)}, u32[]{:S(2)}, u32[]{:S(2)}) collective-permute-start(bf16[3,128,128]{2,1,0:T(8,128)(2,1)} %get-tuple-element.103), channel_id=1, source_target_pairs={{0,7},{1,6},{2,5},{3,4},{4,3},{5,2},{6,1},{7,0},{8,15},{9,14},{10,... | collective-permute-start | bytes 294920 | tf_op jit(solution)/shard_map/ppermute | solution.py:38
  61.1 9.5 %attend.2 = (bf16[128,384]{1,0:T(8,128)(2,1)}, bf16[128,384]{1,0:T(8,128)(2,1)}, bf16[128,384]{1,0:T(8,128)(2,1)}, bf16[128,384]{1,0:T(8,128)(2,1)}, bf16[128,38...) custom-call(s32[1]{0:T(128)} %get-tuple-element.116.frames_ref, ...), custom_call_target="tpu_custom_call" | custom-call | flops 2415919104 | bytes 3145728 | tf_op jit(solution)/shard_map/attend/pallas_call | solution.py:163
  70.8 7.4 %collective-permute-done.32.rest_4_ = bf16[3,128,128]{2,1,0:T(8,128)(2,1)} collective-permute-done((bf16[3,128,128]{2,1,0:T(8,128)(2,1)}, bf16[3,128,128]{2,1,0:T(8,128)(2,1)}, u32[]{:S(2)}, u32[]{:S(2)}) %collective-permute-start.32) | collective-permute-done | bytes 98336 | tf_op jit(solution)/shard_map/ppermute | solution.py:38
  78.2 8.5 %collective-permute-start.23 = (bf16[128,384]{1,0:T(8,128)(2,1)}, bf16[128,384]{1,0:T(8,128)(2,1)S(1)}, u32[]{:S(2)}, u32[]{:S(2)}) collective-permute-start(bf16[128,384]{1,0:T(8,128)(2,1)} %get-tuple-element.84), channel_id=1, source_target_pairs={{0,2},{1,3},{2,0},{3,1},{4,6},{5,7},{6,4},{7,5},{8,10},{9,11},{10,... | collective-permute-start | bytes 294920 | tf_op jit(solution)/shard_map/ppermute | solution.py:38
  87.5 6.1 %attend.3 = (bf16[128,128]{1,0:T(8,128)(2,1)}, bf16[128,128]{1,0:T(8,128)(2,1)}, bf16[128,128]{1,0:T(8,128)(2,1)}, bf16[128,128]{1,0:T(8,128)(2,1)}, bf16[128,12...) custom-call(s32[1]{0:T(128)} %get-tuple-element.116.frames_ref, ...), custom_call_target="tpu_custom_call" | custom-call | flops 805306368 | bytes 1048576 | tf_op jit(solution)/shard_map/attend/pallas_call | solution.py:163
  96.8 1.8 %collective-permute-start.24 = (bf16[128,384]{1,0:T(8,128)(2,1)S(1)}, bf16[128,384]{1,0:T(8,128)(2,1)S(1)}, u32[]{:S(2)}, u32[]{:S(2)}) collective-permute-start(bf16[128,384]{1,0:T(8,128)(2,1)S(1)} %copy-done.32), channel_id=1, source_target_pairs={{0,3},{1,2},{2,1},{3,0},{4,7},{5,6},{6,5},{7,4},{8,11},{9,10},{10,... | collective-permute-start | bytes 294920 | tf_op jit(solution)/shard_map/ppermute | solution.py:38
  99.5 2.0 %collective-permute-start.26 = (bf16[128,384]{1,0:T(8,128)(2,1)S(1)}, bf16[128,384]{1,0:T(8,128)(2,1)S(1)}, u32[]{:S(2)}, u32[]{:S(2)}) collective-permute-start(bf16[128,384]{1,0:T(8,128)(2,1)S(1)} %copy-done.30), channel_id=1, source_target_pairs={{0,5},{1,4},{2,7},{3,6},{4,1},{5,0},{6,3},{7,2},{8,13},{9,12},{10,... | collective-permute-start | bytes 294920 | tf_op jit(solution)/shard_map/ppermute | solution.py:38
  101.4 2.2 %collective-permute-start.27 = (bf16[128,384]{1,0:T(8,128)(2,1)S(1)}, bf16[128,384]{1,0:T(8,128)(2,1)S(1)}, u32[]{:S(2)}, u32[]{:S(2)}) collective-permute-start(bf16[128,384]{1,0:T(8,128)(2,1)S(1)} %copy-done.29), channel_id=1, source_target_pairs={{0,6},{1,7},{2,4},{3,5},{4,2},{5,3},{6,0},{7,1},{8,14},{9,15},{10,... | collective-permute-start | bytes 294920 | tf_op jit(solution)/shard_map/ppermute | solution.py:38
  103.7 1.4 collective-permute-start.28
  105.2 2.5 %collective-permute-start.39 = (bf16[128,128]{1,0:T(8,128)(2,1)}, bf16[128,128]{1,0:T(8,128)(2,1)S(1)}, u32[]{:S(2)}, u32[]{:S(2)}) collective-permute-start(bf16[128,128]{1,0:T(8,128)(2,1)} %get-tuple-element.108), channel_id=1, source_target_pairs={{0,4},{1,5},{2,6},{3,7},{4,0},{5,1},{6,2},{7,3},{8,12},{9,13},{10,... | collective-permute-start | bytes 98312 | tf_op jit(solution)/shard_map/ppermute | solution.py:38
  107.7 7.6 %collective-permute-done.26.rest_5_ = bf16[128,384]{1,0:T(8,128)(2,1)S(1)} collective-permute-done((bf16[128,384]{1,0:T(8,128)(2,1)S(1)}, bf16[128,384]{1,0:T(8,128)(2,1)S(1)}, u32[]{:S(2)}, u32[]{:S(2)}) %collective-permute-start.26) | collective-permute-done | bytes 98336 | tf_op jit(solution)/shard_map/ppermute | solution.py:38
  116.5 2.4 %collective-permute-start.41 = (bf16[128,128]{1,0:T(8,128)(2,1)}, bf16[128,128]{1,0:T(8,128)(2,1)S(1)}, u32[]{:S(2)}, u32[]{:S(2)}) collective-permute-start(bf16[128,128]{1,0:T(8,128)(2,1)} %get-tuple-element.110), channel_id=1, source_target_pairs={{0,6},{1,7},{2,4},{3,5},{4,2},{5,3},{6,0},{7,1},{8,14},{9,15},{10,... | collective-permute-start | bytes 98312 | tf_op jit(solution)/shard_map/ppermute | solution.py:38
  118.8 1.2 fusion.1
  121.3 2.9 %constants.1.const_ref = f32[2,8,256]{2,1,0:T(8,128)} custom-call(f32[3,4096]{1,0:T(4,128)} %bitcast.7, bf16[4096,256]{1,0:T(8,128)(2,1)} %weight_ref.3), custom_call_target="tpu_custom_call" | custom-call | flops 67108864 | bytes 2097152 | tf_op jit(solution)/shard_map/constants/pallas_call | solution.py:282
  124.3 6.1 %project_early.1 = (f32[128,256]{1,0:T(8,128)}, f32[128,128]{1,0:T(8,128)}, f32[128,128]{1,0:T(8,128)}, bf16[128,1024]{1,0:T(8,128)(2,1)}, f32[3,1024]{1,0:T(4,128)}, /*index=5*/bf16[1024,256]{1,0:T(8,128)(2,1)}) custom-call(bf16[1,128,4096]{2,1,0:T(8,128)(2,1)} %h_ref.1, f32[3,4096]{1,0:T(4,128)} %bitcast.8, bf16[4096,256]{1,0:T(8,128)(2,1)} %weight_ref.3, ...), custom_call_target="tpu_custom_call" | custom-call | flops 201326592 | bytes 4194304 | tf_op jit(solution)/shard_map/project_early/pallas_call | solution.py:379
  131.1 3.2 %project_late.1 = bf16[128,256]{1,0:T(8,128)(2,1)S(1)} custom-call(s32[1]{0:T(128)} %get-tuple-element.116.frames_ref, f32[128,256]{1,0:T(8,128)} %get-tuple-element.90.acc_ref, f32[128,128]{1,0:T(8,128)} %get-tuple-element.91.centre_ref, f32[128,128]{1,0:T(8,128)} %get-tuple-element.92.square_ref, bf16[128,1024]{1,0:T(8,128)(2,1)} %get-tuple-element.93.h_ref, ...), custom_call_target="tpu_custom_call" | custom-call | flops 67108864 | bytes 524288 | tf_op jit(solution)/shard_map/project_late/pallas_call | solution.py:452
  134.3 4.2 %conditional.1 = (bf16[128,256]{1,0:T(8,128)(2,1)}) conditional(s32[]{:T(128)} %clamp.3, bf16[128,256]{1,0:T(8,128)(2,1)S(1)} %project_late.1, bf16[128,256]{1,0:T(8,128)(2,1)S(1)} %project_late.1, bf16[128,256]{1,0:T(8,128)(2,1)S(1)} %project_late.1, bf16[128,256]{1,0:T(8,128)(2,1)S(1)} %project_late.1, ...), branch_computations={%region_3.4_spmd, %region_4.5_spmd, %region_5.6_spmd, %region_6.7_... | conditional | bytes 262192 | solution.py:612
  134.6 3.9 %collective-permute-done.14 = bf16[128,256]{1,0:T(8,128)(2,1)} collective-permute-done((bf16[128,256]{1,0:T(8,128)(2,1)S(1)}, bf16[128,256]{1,0:T(8,128)(2,1)}, u32[]{:S(2)}, u32[]{:S(2)}) %collective-permute-start.14) | collective-permute-done | bytes 65568 | tf_op jit(solution)/shard_map/cond/branch_14_fun/ppermute | solution.py:605
  139.3 2.4 %collective-permute-start.43 = (bf16[64,256]{1,0:T(8,128)(2,1)S(1)}, bf16[64,256]{1,0:T(8,128)(2,1)S(1)}, u32[]{:S(2)}, u32[]{:S(2)}) collective-permute-start(bf16[64,256]{1,0:T(8,128)(2,1)S(1)} %get-tuple-element.115), channel_id=1, source_target_pairs={{0,1},{1,0},{2,3},{3,2},{4,5},{5,4},{6,7},{7,6},{8,9},{9,8},{10,11... | collective-permute-start | bytes 98312 | tf_op jit(solution)/shard_map/ppermute | solution.py:632
  141.7 5.5 %collective-permute-start.44 = (bf16[64,256]{1,0:T(8,128)(2,1)S(1)}, bf16[64,256]{1,0:T(8,128)(2,1)S(1)}, u32[]{:S(2)}, u32[]{:S(2)}) collective-permute-start(bf16[64,256]{1,0:T(8,128)(2,1)S(1)} %get-tuple-element.114), channel_id=1, source_target_pairs={{1,2},{3,4},{5,6},{2,1},{4,3},{6,5},{9,10},{11,12},{13,14},{10,9},... | collective-permute-start | bytes 98312 | tf_op jit(solution)/shard_map/ppermute | solution.py:632
  147.2 4.2 %refine_inner.1.inner_ref = f32[128,256]{1,0:T(8,128)} custom-call(bf16[128,256]{1,0:T(8,128)(2,1)} %get-tuple-element.118.mid_ref, bf16[27,256,256]{2,1,0:T(8,128)(2,1)} %bitcast.5), custom_call_target="tpu_custom_call" | custom-call | flops 301989888 | bytes 3735552 | tf_op jit(solution)/shard_map/refine_inner/pallas_call | solution.py:565
  152.1 4.3 %refine_edge.1 = bf16[1,128,256]{2,1,0:T(8,128)(2,1)} custom-call(s32[1]{0:T(128)} %get-tuple-element.117.frames_ref, f32[128,256]{1,0:T(8,128)} %refine_inner.1.inner_ref, bf16[64,256]{1,0:T(8,128)(2,1)} %copy-done.8, bf16[64,256]{1,0:T(8,128)(2,1)} %copy-done.9, bf16[27,256,256]{2,1,0:T(8,128)(2,1)} %bitcast.6), custom_call_target="tpu_custom_call" | custom-call | flops 150994944 | bytes 3735552 | tf_op jit(solution)/shard_map/refine_edge/pallas_call | solution.py:578
  (123 shorter events, 12.0 us)
Async XLA Ops:
  0.0 105.1 %copy-start = (f32[32,3,4096]{2,0,1:T(8,128)S(1)}, f32[32,3,4096]{2,0,1:T(8,128)}, u32[]{:S(2)}) copy-start(f32[32,3,4096]{2,0,1:T(8,128)} %param.31) | copy-start | bytes 4718596
  2.9 20.7 %collective-permute-start.15 = (bf16[3,128,384]{2,1,0:T(8,128)(2,1)}, bf16[3,128,384]{2,1,0:T(8,128)(2,1)S(1)}, u32[]{:S(2)}, u32[]{:S(2)}) collective-permute-start(bf16[3,128,384]{2,1,0:T(8,128)(2,1)} %get-tuple-element.75), channel_id=1, source_target_pairs={{0,1},{1,0},{2,3},{3,2},{4,5},{5,4},{6,7},{7,6},{8,9},{9,8},{10,11... | collective-permute-start | bytes 884744 | tf_op jit(solution)/shard_map/ppermute | solution.py:38
  3.7 20.6 %collective-permute-start.16 = (bf16[3,128,384]{2,1,0:T(8,128)(2,1)}, bf16[3,128,384]{2,1,0:T(8,128)(2,1)S(1)}, u32[]{:S(2)}, u32[]{:S(2)}) collective-permute-start(bf16[3,128,384]{2,1,0:T(8,128)(2,1)} %get-tuple-element.76), channel_id=1, source_target_pairs={{0,2},{1,3},{2,0},{3,1},{4,6},{5,7},{6,4},{7,5},{8,10},{9,11},{10,... | collective-permute-start | bytes 884744 | tf_op jit(solution)/shard_map/ppermute | solution.py:38
  7.0 2.2 %collective-permute-start.29 = (bf16[3,128,128]{2,1,0:T(8,128)(2,1)}, bf16[3,128,128]{2,1,0:T(8,128)(2,1)S(1)}, u32[]{:S(2)}, u32[]{:S(2)}) collective-permute-start(bf16[3,128,128]{2,1,0:T(8,128)(2,1)} %get-tuple-element.97), channel_id=1, source_target_pairs={{0,1},{1,0},{2,3},{3,2},{4,5},{5,4},{6,7},{7,6},{8,9},{9,8},{10,11... | collective-permute-start | bytes 294920 | tf_op jit(solution)/shard_map/ppermute | solution.py:38
  7.4 13.4 %collective-permute-start.30 = (bf16[3,128,128]{2,1,0:T(8,128)(2,1)}, bf16[3,128,128]{2,1,0:T(8,128)(2,1)S(1)}, u32[]{:S(2)}, u32[]{:S(2)}) collective-permute-start(bf16[3,128,128]{2,1,0:T(8,128)(2,1)} %get-tuple-element.98), channel_id=1, source_target_pairs={{0,2},{1,3},{2,0},{3,1},{4,6},{5,7},{6,4},{7,5},{8,10},{9,11},{10,... | collective-permute-start | bytes 294920 | tf_op jit(solution)/shard_map/ppermute | solution.py:38
  7.6 21.9 %collective-permute-start.17 = (bf16[3,128,384]{2,1,0:T(8,128)(2,1)}, bf16[3,128,384]{2,1,0:T(8,128)(2,1)S(1)}, u32[]{:S(2)}, u32[]{:S(2)}) collective-permute-start(bf16[3,128,384]{2,1,0:T(8,128)(2,1)} %get-tuple-element.77), channel_id=1, source_target_pairs={{0,3},{1,2},{2,1},{3,0},{4,7},{5,6},{6,5},{7,4},{8,11},{9,10},{10,... | collective-permute-start | bytes 884744 | tf_op jit(solution)/shard_map/ppermute | solution.py:38
  9.2 21.7 %collective-permute-start.18 = (bf16[3,128,384]{2,1,0:T(8,128)(2,1)}, bf16[3,128,384]{2,1,0:T(8,128)(2,1)}, u32[]{:S(2)}, u32[]{:S(2)}) collective-permute-start(bf16[3,128,384]{2,1,0:T(8,128)(2,1)} %get-tuple-element.78), channel_id=1, source_target_pairs={{0,4},{1,5},{2,6},{3,7},{4,0},{5,1},{6,2},{7,3},{8,12},{9,13},{10,... | collective-permute-start | bytes 884744 | tf_op jit(solution)/shard_map/ppermute | solution.py:38
  20.8 36.3 %collective-permute-start.19 = (bf16[3,128,384]{2,1,0:T(8,128)(2,1)S(1)}, bf16[3,128,384]{2,1,0:T(8,128)(2,1)}, u32[]{:S(2)}, u32[]{:S(2)}) collective-permute-start(bf16[3,128,384]{2,1,0:T(8,128)(2,1)S(1)} %copy-done.25), channel_id=1, source_target_pairs={{0,5},{1,4},{2,7},{3,6},{4,1},{5,0},{6,3},{7,2},{8,13},{9,12},{10,... | collective-permute-start | bytes 884744 | tf_op jit(solution)/shard_map/ppermute | solution.py:38
  23.7 33.4 %collective-permute-start.20 = (bf16[3,128,384]{2,1,0:T(8,128)(2,1)S(1)}, bf16[3,128,384]{2,1,0:T(8,128)(2,1)}, u32[]{:S(2)}, u32[]{:S(2)}) collective-permute-start(bf16[3,128,384]{2,1,0:T(8,128)(2,1)S(1)} %copy-done.23), channel_id=1, source_target_pairs={{0,6},{1,7},{2,4},{3,5},{4,2},{5,3},{6,0},{7,1},{8,14},{9,15},{10,... | collective-permute-start | bytes 884744 | tf_op jit(solution)/shard_map/ppermute | solution.py:38
  24.2 33.9 %collective-permute-start.21 = (bf16[3,128,384]{2,1,0:T(8,128)(2,1)S(1)}, bf16[3,128,384]{2,1,0:T(8,128)(2,1)}, u32[]{:S(2)}, u32[]{:S(2)}) collective-permute-start(bf16[3,128,384]{2,1,0:T(8,128)(2,1)S(1)} %copy-done.22), channel_id=1, source_target_pairs={{0,7},{1,6},{2,5},{3,4},{4,3},{5,2},{6,1},{7,0},{8,15},{9,14},{10,... | collective-permute-start | bytes 884744 | tf_op jit(solution)/shard_map/ppermute | solution.py:38
  29.5 41.1 %collective-permute-start.31 = (bf16[3,128,128]{2,1,0:T(8,128)(2,1)}, bf16[3,128,128]{2,1,0:T(8,128)(2,1)}, u32[]{:S(2)}, u32[]{:S(2)}) collective-permute-start(bf16[3,128,128]{2,1,0:T(8,128)(2,1)} %get-tuple-element.99), channel_id=1, source_target_pairs={{0,3},{1,2},{2,1},{3,0},{4,7},{5,6},{6,5},{7,4},{8,11},{9,10},{10,... | collective-permute-start | bytes 294920 | tf_op jit(solution)/shard_map/ppermute | solution.py:38
  30.9 47.3 %collective-permute-start.32 = (bf16[3,128,128]{2,1,0:T(8,128)(2,1)}, bf16[3,128,128]{2,1,0:T(8,128)(2,1)}, u32[]{:S(2)}, u32[]{:S(2)}) collective-permute-start(bf16[3,128,128]{2,1,0:T(8,128)(2,1)} %get-tuple-element.100), channel_id=1, source_target_pairs={{0,4},{1,5},{2,6},{3,7},{4,0},{5,1},{6,2},{7,3},{8,12},{9,13},{10,... | collective-permute-start | bytes 294920 | tf_op jit(solution)/shard_map/ppermute | solution.py:38
  57.1 29.6 %collective-permute-start.33 = (bf16[3,128,128]{2,1,0:T(8,128)(2,1)}, bf16[3,128,128]{2,1,0:T(8,128)(2,1)S(1)}, u32[]{:S(2)}, u32[]{:S(2)}) collective-permute-start(bf16[3,128,128]{2,1,0:T(8,128)(2,1)} %get-tuple-element.101), channel_id=1, source_target_pairs={{0,5},{1,4},{2,7},{3,6},{4,1},{5,0},{6,3},{7,2},{8,13},{9,12},{10,... | collective-permute-start | bytes 294920 | tf_op jit(solution)/shard_map/ppermute | solution.py:38
  57.1 29.6 %collective-permute-start.34 = (bf16[3,128,128]{2,1,0:T(8,128)(2,1)}, bf16[3,128,128]{2,1,0:T(8,128)(2,1)S(1)}, u32[]{:S(2)}, u32[]{:S(2)}) collective-permute-start(bf16[3,128,128]{2,1,0:T(8,128)(2,1)} %get-tuple-element.102), channel_id=1, source_target_pairs={{0,6},{1,7},{2,4},{3,5},{4,2},{5,3},{6,0},{7,1},{8,14},{9,15},{10,... | collective-permute-start | bytes 294920 | tf_op jit(solution)/shard_map/ppermute | solution.py:38
  58.2 28.6 %collective-permute-start.35 = (bf16[3,128,128]{2,1,0:T(8,128)(2,1)}, bf16[3,128,128]{2,1,0:T(8,128)(2,1)S(1)}, u32[]{:S(2)}, u32[]{:S(2)}) collective-permute-start(bf16[3,128,128]{2,1,0:T(8,128)(2,1)} %get-tuple-element.103), channel_id=1, source_target_pairs={{0,7},{1,6},{2,5},{3,4},{4,3},{5,2},{6,1},{7,0},{8,15},{9,14},{10,... | collective-permute-start | bytes 294920 | tf_op jit(solution)/shard_map/ppermute | solution.py:38
  70.7 30.7 %collective-permute-start.22 = (bf16[128,384]{1,0:T(8,128)(2,1)}, bf16[128,384]{1,0:T(8,128)(2,1)S(1)}, u32[]{:S(2)}, u32[]{:S(2)}) collective-permute-start(bf16[128,384]{1,0:T(8,128)(2,1)} %get-tuple-element.83), channel_id=1, source_target_pairs={{0,1},{1,0},{2,3},{3,2},{4,5},{5,4},{6,7},{7,6},{8,9},{9,8},{10,11... | collective-permute-start | bytes 294920 | tf_op jit(solution)/shard_map/ppermute | solution.py:38
  78.2 25.5 %collective-permute-start.23 = (bf16[128,384]{1,0:T(8,128)(2,1)}, bf16[128,384]{1,0:T(8,128)(2,1)S(1)}, u32[]{:S(2)}, u32[]{:S(2)}) collective-permute-start(bf16[128,384]{1,0:T(8,128)(2,1)} %get-tuple-element.84), channel_id=1, source_target_pairs={{0,2},{1,3},{2,0},{3,1},{4,6},{5,7},{6,4},{7,5},{8,10},{9,11},{10,... | collective-permute-start | bytes 294920 | tf_op jit(solution)/shard_map/ppermute | solution.py:38
  93.6 5.0 %collective-permute-start.36 = (bf16[128,128]{1,0:T(8,128)(2,1)}, bf16[128,128]{1,0:T(8,128)(2,1)S(1)}, u32[]{:S(2)}, u32[]{:S(2)}) collective-permute-start(bf16[128,128]{1,0:T(8,128)(2,1)} %get-tuple-element.105), channel_id=1, source_target_pairs={{0,1},{1,0},{2,3},{3,2},{4,5},{5,4},{6,7},{7,6},{8,9},{9,8},{10,11... | collective-permute-start | bytes 98312 | tf_op jit(solution)/shard_map/ppermute | solution.py:38
  94.4 5.1 %collective-permute-start.37 = (bf16[128,128]{1,0:T(8,128)(2,1)}, bf16[128,128]{1,0:T(8,128)(2,1)S(1)}, u32[]{:S(2)}, u32[]{:S(2)}) collective-permute-start(bf16[128,128]{1,0:T(8,128)(2,1)} %get-tuple-element.106), channel_id=1, source_target_pairs={{0,2},{1,3},{2,0},{3,1},{4,6},{5,7},{6,4},{7,5},{8,10},{9,11},{10,... | collective-permute-start | bytes 98312 | tf_op jit(solution)/shard_map/ppermute | solution.py:38
  96.8 8.3 %collective-permute-start.24 = (bf16[128,384]{1,0:T(8,128)(2,1)S(1)}, bf16[128,384]{1,0:T(8,128)(2,1)S(1)}, u32[]{:S(2)}, u32[]{:S(2)}) collective-permute-start(bf16[128,384]{1,0:T(8,128)(2,1)S(1)} %copy-done.32), channel_id=1, source_target_pairs={{0,3},{1,2},{2,1},{3,0},{4,7},{5,6},{6,5},{7,4},{8,11},{9,10},{10,... | collective-permute-start | bytes 294920 | tf_op jit(solution)/shard_map/ppermute | solution.py:38
  98.6 6.6 %collective-permute-start.25 = (bf16[128,384]{1,0:T(8,128)(2,1)S(1)}, bf16[128,384]{1,0:T(8,128)(2,1)S(1)}, u32[]{:S(2)}, u32[]{:S(2)}) collective-permute-start(bf16[128,384]{1,0:T(8,128)(2,1)S(1)} %copy-done.31), channel_id=1, source_target_pairs={{0,4},{1,5},{2,6},{3,7},{4,0},{5,1},{6,2},{7,3},{8,12},{9,13},{10,... | collective-permute-start | bytes 294920 | tf_op jit(solution)/shard_map/ppermute | solution.py:38
  99.5 15.8 %collective-permute-start.26 = (bf16[128,384]{1,0:T(8,128)(2,1)S(1)}, bf16[128,384]{1,0:T(8,128)(2,1)S(1)}, u32[]{:S(2)}, u32[]{:S(2)}) collective-permute-start(bf16[128,384]{1,0:T(8,128)(2,1)S(1)} %copy-done.30), channel_id=1, source_target_pairs={{0,5},{1,4},{2,7},{3,6},{4,1},{5,0},{6,3},{7,2},{8,13},{9,12},{10,... | collective-permute-start | bytes 294920 | tf_op jit(solution)/shard_map/ppermute | solution.py:38
  101.4 15.0 %collective-permute-start.27 = (bf16[128,384]{1,0:T(8,128)(2,1)S(1)}, bf16[128,384]{1,0:T(8,128)(2,1)S(1)}, u32[]{:S(2)}, u32[]{:S(2)}) collective-permute-start(bf16[128,384]{1,0:T(8,128)(2,1)S(1)} %copy-done.29), channel_id=1, source_target_pairs={{0,6},{1,7},{2,4},{3,5},{4,2},{5,3},{6,0},{7,1},{8,14},{9,15},{10,... | collective-permute-start | bytes 294920 | tf_op jit(solution)/shard_map/ppermute | solution.py:38
  103.7 15.2 %collective-permute-start.28 = (bf16[128,384]{1,0:T(8,128)(2,1)S(1)}, bf16[128,384]{1,0:T(8,128)(2,1)S(1)}, u32[]{:S(2)}, u32[]{:S(2)}) collective-permute-start(bf16[128,384]{1,0:T(8,128)(2,1)S(1)} %copy-done.28), channel_id=1, source_target_pairs={{0,7},{1,6},{2,5},{3,4},{4,3},{5,2},{6,1},{7,0},{8,15},{9,14},{10,... | collective-permute-start | bytes 294920 | tf_op jit(solution)/shard_map/ppermute | solution.py:38
  105.1 25.3 %collective-permute-start.38 = (bf16[128,128]{1,0:T(8,128)(2,1)}, bf16[128,128]{1,0:T(8,128)(2,1)S(1)}, u32[]{:S(2)}, u32[]{:S(2)}) collective-permute-start(bf16[128,128]{1,0:T(8,128)(2,1)} %get-tuple-element.107), channel_id=1, source_target_pairs={{0,3},{1,2},{2,1},{3,0},{4,7},{5,6},{6,5},{7,4},{8,11},{9,10},{10,... | collective-permute-start | bytes 98312 | tf_op jit(solution)/shard_map/ppermute | solution.py:38
  105.2 25.2 %collective-permute-start.39 = (bf16[128,128]{1,0:T(8,128)(2,1)}, bf16[128,128]{1,0:T(8,128)(2,1)S(1)}, u32[]{:S(2)}, u32[]{:S(2)}) collective-permute-start(bf16[128,128]{1,0:T(8,128)(2,1)} %get-tuple-element.108), channel_id=1, source_target_pairs={{0,4},{1,5},{2,6},{3,7},{4,0},{5,1},{6,2},{7,3},{8,12},{9,13},{10,... | collective-permute-start | bytes 98312 | tf_op jit(solution)/shard_map/ppermute | solution.py:38
  115.3 15.2 %collective-permute-start.40 = (bf16[128,128]{1,0:T(8,128)(2,1)}, bf16[128,128]{1,0:T(8,128)(2,1)S(1)}, u32[]{:S(2)}, u32[]{:S(2)}) collective-permute-start(bf16[128,128]{1,0:T(8,128)(2,1)} %get-tuple-element.109), channel_id=1, source_target_pairs={{0,5},{1,4},{2,7},{3,6},{4,1},{5,0},{6,3},{7,2},{8,13},{9,12},{10,... | collective-permute-start | bytes 98312 | tf_op jit(solution)/shard_map/ppermute | solution.py:38
  116.5 14.0 %collective-permute-start.41 = (bf16[128,128]{1,0:T(8,128)(2,1)}, bf16[128,128]{1,0:T(8,128)(2,1)S(1)}, u32[]{:S(2)}, u32[]{:S(2)}) collective-permute-start(bf16[128,128]{1,0:T(8,128)(2,1)} %get-tuple-element.110), channel_id=1, source_target_pairs={{0,6},{1,7},{2,4},{3,5},{4,2},{5,3},{6,0},{7,1},{8,14},{9,15},{10,... | collective-permute-start | bytes 98312 | tf_op jit(solution)/shard_map/ppermute | solution.py:38
  118.8 11.7 %collective-permute-start.42 = (bf16[128,128]{1,0:T(8,128)(2,1)}, bf16[128,128]{1,0:T(8,128)(2,1)S(1)}, u32[]{:S(2)}, u32[]{:S(2)}) collective-permute-start(bf16[128,128]{1,0:T(8,128)(2,1)} %get-tuple-element.111), channel_id=1, source_target_pairs={{0,7},{1,6},{2,5},{3,4},{4,3},{5,2},{6,1},{7,0},{8,15},{9,14},{10,... | collective-permute-start | bytes 98312 | tf_op jit(solution)/shard_map/ppermute | solution.py:38
  134.4 4.2 %collective-permute-start.14 = (bf16[128,256]{1,0:T(8,128)(2,1)S(1)}, bf16[128,256]{1,0:T(8,128)(2,1)}, u32[]{:S(2)}, u32[]{:S(2)}) collective-permute-start(bf16[128,256]{1,0:T(8,128)(2,1)S(1)} %param.14), channel_id=1, source_target_pairs={{0,24},{8,16},{16,0},{24,8},{1,25},{9,17},{17,1},{25,9},{2,26},{10... | collective-permute-start | bytes 196616 | tf_op jit(solution)/shard_map/cond/branch_14_fun/ppermute | solution.py:605
  139.3 12.1 %collective-permute-start.43 = (bf16[64,256]{1,0:T(8,128)(2,1)S(1)}, bf16[64,256]{1,0:T(8,128)(2,1)S(1)}, u32[]{:S(2)}, u32[]{:S(2)}) collective-permute-start(bf16[64,256]{1,0:T(8,128)(2,1)S(1)} %get-tuple-element.115), channel_id=1, source_target_pairs={{0,1},{1,0},{2,3},{3,2},{4,5},{5,4},{6,7},{7,6},{8,9},{9,8},{10,11... | collective-permute-start | bytes 98312 | tf_op jit(solution)/shard_map/ppermute | solution.py:632
  141.7 9.7 %collective-permute-start.44 = (bf16[64,256]{1,0:T(8,128)(2,1)S(1)}, bf16[64,256]{1,0:T(8,128)(2,1)S(1)}, u32[]{:S(2)}, u32[]{:S(2)}) collective-permute-start(bf16[64,256]{1,0:T(8,128)(2,1)S(1)} %get-tuple-element.114), channel_id=1, source_target_pairs={{1,2},{3,4},{5,6},{2,1},{4,3},{6,5},{9,10},{11,12},{13,14},{10,9},... | collective-permute-start | bytes 98312 | tf_op jit(solution)/shard_map/ppermute | solution.py:632
  (37 other events, 773.4 us)
where the time goes:
time: 157 us; the launch traced here: 156 us
  waiting for transfers between devices  54 us (34%)
  starting transfers between devices  49.6 us (32%)
  Pallas kernels  41.3 us (26%)
  between operations  4.83 us (3%)
  local copies, waits for them, and re-layouts  4.74 us (3%)
  other arithmetic  1.89 us (1%)
    ppermute x28, waiting for transfers between devices, exchange(): out[step] = lax.ppermute(pieces[step], axis, ring(step, count))  50.1 us
    ppermute x28, starting transfers between devices, exchange(): out[step] = lax.ppermute(pieces[step], axis, ring(step, count))  41.5 us
    pallas_call x2, Pallas kernels, attend(): pl.pallas_call(functools.partial(attend_kernel, count, heads, block_rows)...  15.7 us
    pallas_call x1, Pallas kernels, project_early(): pl.pallas_call(functools.partial(early_kernel, count, head_cols), out_sha...  6.13 us
    ppermute x1, starting transfers between devices, halos(): lax.ppermute(crossing, 'ctx', outer)  5.48 us
    pallas_call x2, Pallas kernels, pack(): pl.pallas_call(functools.partial(pack_kernel, count, kinds, head_cols, fi...  4.88 us
    pallas_call x1, Pallas kernels, refine(): pl.pallas_call(edge_kernel, out_shape=jax.ShapeDtypeStruct((1, rows, chan...  4.28 us
    pallas_call x1, Pallas kernels, refine(): pl.pallas_call(inner_kernel, out_shape=jax.ShapeDtypeStruct((rows, channe...  4.22 us
  transfers between devices with their start and end apart: 31, of which 5 were waited for; matrix products, arithmetic and copies ran while one was open for 2% of the time, Pallas kernels for 20%

commit v1 on v0

--- a/solution.py
+++ b/solution.py
@@ -11,6 +11,7 @@
 
 
 HEADS = 32
+VMEM_BYTES = 67043328
 HH = 8
 WW = 8
 
@@ -81,6 +82,7 @@
         cost_estimate=pl.CostEstimate(
             flops=0, bytes_accessed=4 * kinds * count * rows * width, transcendentals=0
         ),
+        compiler_params=pltpu.CompilerParams(vmem_limit_bytes=VMEM_BYTES),
         name="pack",
     )(*sources)
 
@@ -149,7 +151,7 @@
             result[here, lanes] = (both[:, :size] / both[:, size:]).astype(result.dtype)
         return carry
 
-    lax.fori_loop(0, seq // block_rows, block, 0)
+    lax.fori_loop(0, seq // block_rows, block, 0, unroll=4)
     for step in range(count):
         save(step).start()
     for step in range(count):
@@ -179,6 +181,7 @@
             bytes_accessed=8 * seq * width,
             transcendentals=seq * seq * heads,
         ),
+        compiler_params=pltpu.CompilerParams(vmem_limit_bytes=VMEM_BYTES),
         name="attend",
     )(frames, *pieces)
 
@@ -258,6 +261,7 @@
             bytes_accessed=4 * rows * model + 2 * model * channels,
             transcendentals=0,
         ),
+        compiler_params=pltpu.CompilerParams(vmem_limit_bytes=VMEM_BYTES),
         name="project",
     )(frames, hidden_state, modulation, down_weight, *pieces)
 
@@ -287,6 +291,7 @@
         cost_estimate=pl.CostEstimate(
             flops=64 * model * channels, bytes_accessed=2 * model * channels, transcendentals=0
         ),
+        compiler_params=pltpu.CompilerParams(vmem_limit_bytes=VMEM_BYTES),
         name="constants",
     )(mod_rows, down_weight)
 
@@ -404,14 +409,15 @@
             bytes_accessed=4 * rows * model + 2 * model * channels,
             transcendentals=0,
         ),
+        compiler_params=pltpu.CompilerParams(vmem_limit_bytes=VMEM_BYTES),
         name="project_early",
     )(hidden_state, mod_rows, down_weight, *pieces)
 
 
-def late_kernel(
-    count, early, frames_ref, acc_ref, centre_ref, square_ref, h_ref, mod_ref, weight_ref, const_ref, *rest
-):
-    pieces, (out_ref, attended, in_sem) = rest[:count], rest[count:]
+def late_kernel(count, early, frames_ref, *rest):
+    sources, pieces, rest = rest[:7], rest[7 : 7 + count], rest[7 + count :]
+    out_ref, attended, held, in_sem, held_sem = rest[0], rest[1], rest[2:9], rest[9], rest[10]
+    acc_ref, centre_ref, square_ref, h_ref, mod_ref, weight_ref, const_ref = held
     rows, width = pieces[0].shape
     late = count * width
     model = early + late
@@ -421,8 +427,15 @@
             pieces[step], attended.at[:, pl.ds(step * width, width)], in_sem.at[step]
         )
 
+    def hold(which):
+        return pltpu.make_async_copy(sources[which], held[which], held_sem.at[which])
+
     for step in range(count):
         load(step).start()
+    for which in (3, 4, 1, 2, 5, 0, 6):
+        hold(which).start()
+    for which in (3, 4, 1, 2):
+        hold(which).wait()
     for step in range(count):
         load(step).wait()
     wide = (
@@ -431,13 +444,15 @@
         .astype(jnp.float32)
     )
     first = centre_ref[:, :1]
+    scaled = ((wide - first) * (1.0 + mod_ref[1:2, :])).astype(jnp.bfloat16)
+    for which in (5, 0, 6):
+        hold(which).wait()
+    total = acc_ref[...] + jnp.dot(scaled, weight_ref[...], preferred_element_type=jnp.float32)
     own = jnp.mean(wide, axis=-1, keepdims=True)
     square = jnp.sum(jnp.square(wide - own), axis=-1, keepdims=True)
     gap = own - first
     centre = first + gap * (late / model)
     spread = (square_ref[:, :1] + square + gap * gap * (early * late / model)) / model
-    scaled = ((wide - first) * (1.0 + mod_ref[1:2, :])).astype(jnp.bfloat16)
-    total = acc_ref[...] + jnp.dot(scaled, weight_ref[...], preferred_element_type=jnp.float32)
     total = total + (first - centre) * const_ref[0, :1, :]
     total = total * lax.rsqrt(spread + 1e-06) + const_ref[1, :1, :]
     token = lax.axis_index("ctx") * rows + lax.broadcasted_iota(jnp.int32, (rows, 1), 0)
@@ -448,118 +463,111 @@
     rows, width = pieces[0].shape
     channels = consts.shape[-1]
     hbm = pl.BlockSpec(memory_space=pltpu.HBM)
-    vmem = pl.BlockSpec(memory_space=pltpu.VMEM)
+    sources = (*early, consts)
     return pl.pallas_call(
         functools.partial(late_kernel, count, model - count * width),
         out_shape=jax.ShapeDtypeStruct((rows, channels), jnp.bfloat16),
-        in_specs=[pl.BlockSpec(memory_space=pltpu.SMEM)] + [vmem] * 7 + [hbm] * count,
-        out_specs=vmem,
-        scratch_shapes=[
-            pltpu.VMEM((rows, count * width), jnp.bfloat16),
-            pltpu.SemaphoreType.DMA((count,)),
-        ],
+        in_specs=[pl.BlockSpec(memory_space=pltpu.SMEM)] + [hbm] * (7 + count),
+        out_specs=pl.BlockSpec(memory_space=pltpu.VMEM),
+        scratch_shapes=[pltpu.VMEM((rows, count * width), jnp.bfloat16)]
+        + [pltpu.VMEM(source.shape, source.dtype) for source in sources]
+        + [pltpu.SemaphoreType.DMA((count,)), pltpu.SemaphoreType.DMA((7,))],
         cost_estimate=pl.CostEstimate(
             flops=2 * rows * count * width * channels,
             bytes_accessed=4 * rows * count * width,
             transcendentals=0,
         ),
+        compiler_params=pltpu.CompilerParams(vmem_limit_bytes=VMEM_BYTES),
         name="project_late",
-    )(frames, *early, consts, *pieces)
-
-
-def shifted_frames(frames, channels):
+    )(frames, *sources, *pieces)
+
+
+def gather_taps(frames, taps):
     cells = HH * WW
+    channels = frames[0].shape[1]
     column = lax.broadcasted_iota(jnp.int32, (cells, 1), 0) % WW
     blank = jnp.zeros((WW, channels), jnp.float32)
-    shifted = []
-    for offset in (-1, 0, 1):
-        moved = []
-        for frame in frames:
-            cell = frame.astype(jnp.float32)
+    for number, frame in enumerate(frames):
+        wide = frame.astype(jnp.float32)
+        for across, offset in enumerate((-1, 0, 1)):
+            cell = wide
             if offset:
-                cell = pltpu.roll(cell, (-offset) % cells, 0)
                 inside = (column + offset >= 0) & (column + offset < WW)
-                cell = jnp.where(inside, cell, 0.0)
-            moved.append(jnp.concatenate([blank, cell, blank], axis=0))
-        shifted.append(moved)
-    return shifted
-
-
-def window(shifted, across, down):
+                cell = jnp.where(inside, pltpu.roll(wide, (-offset) % cells, 0), 0.0)
+            cell = jnp.concatenate([blank, cell, blank], axis=0)
+            for down in range(3):
+                taps[
+                    pl.ds(number * cells, cells), pl.ds((down * 3 + across) * channels, channels)
+                ] = cell[down * WW : down * WW + cells].astype(jnp.bfloat16)
+
+
+def inner_kernel(mid_ref, weight_ref, out_ref, taps, weight, sem):
     cells = HH * WW
-    return [f[down * WW : down * WW + cells].astype(jnp.bfloat16) for f in shifted[across]]
-
-
-def inner_kernel(mid_ref, weight_ref, out_ref, weight, sem):
-    cells = HH * WW
-    rows, channels = mid_ref.shape
-    copy = pltpu.make_async_copy(weight_ref, weight, sem)
-    copy.start()
-    frames = [mid_ref[pl.ds(start, cells), :] for start in range(0, rows, cells)]
-    shifted = shifted_frames(frames, channels)
-    copy.wait()
-    totals = [frame.astype(jnp.float32) for frame in frames]
-    centre = jnp.zeros((rows, channels), jnp.float32)
-    for down in range(3):
-        for across in range(3):
-            picked = window(shifted, across, down)
-            centre += jnp.dot(
-                jnp.concatenate(picked, axis=0),
-                weight[(3 + down) * 3 + across],
-                preferred_element_type=jnp.float32,
-            )
-            for target in range(len(frames)):
-                for ahead in (0, 2):
-                    if 0 <= target + ahead - 1 < len(frames):
-                        totals[target] += jnp.dot(
-                            picked[target + ahead - 1],
-                            weight[(ahead * 3 + down) * 3 + across],
-                            preferred_element_type=jnp.float32,
-                        )
-    for target in range(len(frames)):
-        here = pl.ds(target * cells, cells)
-        out_ref[here, :] = totals[target] + centre[target * cells : (target + 1) * cells]
-
-
-def edge_kernel(frames_ref, inner_ref, even_ref, odd_ref, weight_ref, out_ref, weight, sem):
+    rows, _ = mid_ref.shape
+
+    def fetch(ahead):
+        return pltpu.make_async_copy(weight_ref.at[ahead], weight.at[ahead], sem.at[ahead])
+
+    for ahead in (1, 0, 2):
+        fetch(ahead).start()
+    gather_taps([mid_ref[pl.ds(start, cells), :] for start in range(0, rows, cells)], taps)
+    fetch(1).wait()
+    out_ref[...] = mid_ref[...].astype(jnp.float32) + jnp.dot(
+        taps[...], weight[1], preferred_element_type=jnp.float32
+    )
+    fetch(0).wait()
+    fetch(2).wait()
+    if rows > cells:
+        rest = rows - cells
+        out_ref[pl.ds(cells, rest), :] += jnp.dot(
+            taps[pl.ds(0, rest), :], weight[0], preferred_element_type=jnp.float32
+        )
+        out_ref[pl.ds(0, rest), :] += jnp.dot(
+            taps[pl.ds(cells, rest), :], weight[2], preferred_element_type=jnp.float32
+        )
+
+
+def edge_kernel(frames_ref, inner_ref, even_ref, odd_ref, weight_ref, out_ref, taps, weight, sem):
     cells = HH * WW
     rows, channels = inner_ref.shape
     me = lax.axis_index("ctx")
 
-    def fetch(ahead):
-        return pltpu.make_async_copy(
-            weight_ref.at[pl.ds(ahead * 9, 9)], weight.at[ahead // 2], sem.at[ahead // 2]
-        )
+    def fetch(side):
+        return pltpu.make_async_copy(weight_ref.at[2 * side], weight.at[side], sem.at[side])
 
     fetch(0).start()
-    fetch(2).start()
+    fetch(1).start()
     odd = lax.rem(me, 2) == 1
     low = jnp.where(odd, even_ref[...], odd_ref[...])
     high = jnp.where(odd, odd_ref[...], even_ref[...])
-    shifted = shifted_frames([low, high], channels)
-    first = inner_ref[pl.ds(0, cells), :]
-    last = jnp.zeros((cells, channels), jnp.float32)
-    fetch(0).wait()
-    fetch(2).wait()
-    for down in range(3):
-        for across in range(3):
-            below, above = window(shifted, across, down)
-            first += jnp.dot(
-                below, weight[0, down * 3 + across], preferred_element_type=jnp.float32
+    gather_taps([low, high], taps)
+    token = me * rows + lax.broadcasted_iota(jnp.int32, (rows, 1), 0)
+    keep = token < frames_ref[0] * cells
+    sides = []
+    for side in range(2):
+        fetch(side).wait()
+        sides.append(
+            jnp.dot(
+                taps[pl.ds(side * cells, cells), :],
+                weight[side],
+                preferred_element_type=jnp.float32,
             )
-            last += jnp.dot(
-                above, weight[1, down * 3 + across], preferred_element_type=jnp.float32
-            )
-    blank = jnp.zeros((rows - cells, channels), jnp.float32)
-    total = jnp.concatenate([first, inner_ref[pl.ds(cells, rows - cells), :]], axis=0)
-    total = total + jnp.concatenate([blank, last], axis=0)
-    token = me * rows + lax.broadcasted_iota(jnp.int32, (rows, 1), 0)
-    out_ref[0] = jnp.where(token < frames_ref[0] * cells, total, 0.0).astype(out_ref.dtype)
+        )
+    if rows > cells:
+        blank = jnp.zeros((rows - cells, channels), jnp.float32)
+        total = (
+            inner_ref[...]
+            + jnp.concatenate([sides[0], blank], axis=0)
+            + jnp.concatenate([blank, sides[1]], axis=0)
+        )
+    else:
+        total = inner_ref[...] + sides[0] + sides[1]
+    out_ref[0] = jnp.where(keep, total, 0.0).astype(out_ref.dtype)
 
 
 def refine(frames, mid, even, odd, conv_weight):
     rows, channels = mid.shape
-    taps = conv_weight.reshape(-1, channels, channels)
+    taps = conv_weight.reshape(3, 9 * channels, channels)
     hbm = pl.BlockSpec(memory_space=pltpu.HBM)
     vmem = pl.BlockSpec(memory_space=pltpu.VMEM)
     inner = pl.pallas_call(
@@ -567,12 +575,17 @@
         out_shape=jax.ShapeDtypeStruct((rows, channels), jnp.float32),
         in_specs=[vmem, hbm],
         out_specs=vmem,
-        scratch_shapes=[pltpu.VMEM(taps.shape, taps.dtype), pltpu.SemaphoreType.DMA],
+        scratch_shapes=[
+            pltpu.VMEM((rows, 9 * channels), jnp.bfloat16),
+            pltpu.VMEM(taps.shape, taps.dtype),
+            pltpu.SemaphoreType.DMA((3,)),
+        ],
         cost_estimate=pl.CostEstimate(
             flops=36 * rows * channels * channels,
             bytes_accessed=2 * taps.size + 6 * rows * channels,
             transcendentals=0,
         ),
+        compiler_params=pltpu.CompilerParams(vmem_limit_bytes=VMEM_BYTES),
         name="refine_inner",
     )(mid, taps)
     return pl.pallas_call(
@@ -581,7 +594,8 @@
         in_specs=[pl.BlockSpec(memory_space=pltpu.SMEM)] + [vmem] * 3 + [hbm],
         out_specs=vmem,
         scratch_shapes=[
-            pltpu.VMEM((2, 9) + taps.shape[1:], taps.dtype),
+            pltpu.VMEM((2 * HH * WW, 9 * channels), jnp.bfloat16),
+            pltpu.VMEM((2,) + taps.shape[1:], taps.dtype),
             pltpu.SemaphoreType.DMA((2,)),
         ],
         cost_estimate=pl.CostEstimate(
@@ -589,6 +603,7 @@
             bytes_accessed=2 * taps.size + 6 * rows * channels,
             transcendentals=0,
         ),
+        compiler_params=pltpu.CompilerParams(vmem_limit_bytes=VMEM_BYTES),
         name="refine_edge",
     )(frames, inner, even, odd, taps)
 

time: 157 us -> 154 us (0.981)
  the two profiles are of different devices: /device:TPU:5 before, /device:TPU:1 now
where the time goes in v1:
time: 154 us; the launch traced here: 153 us
  waiting for transfers between devices  51.9 us (34%)
  starting transfers between devices  49.1 us (32%)
  Pallas kernels  37.7 us (24%)
  local copies, waits for them, and re-layouts  5.8 us (4%)
  between operations  4.92 us (3%)
  other arithmetic  3.45 us (2%)
    ppermute x28, waiting for transfers between devices, exchange(): out[step] = lax.ppermute(pieces[step], axis, ring(step, count))  50.3 us
    ppermute x28, starting transfers between devices, exchange(): out[step] = lax.ppermute(pieces[step], axis, ring(step, count))  40 us
    pallas_call x2, Pallas kernels, attend(): pl.pallas_call(functools.partial(attend_kernel, count, heads, block_rows)...  12.3 us
    pallas_call x1, Pallas kernels, project_early(): pl.pallas_call(functools.partial(early_kernel, count, head_cols), out_sha...  6.06 us
    ppermute x1, starting transfers between devices, halos(): lax.ppermute(crossing, 'ctx', outer)  4.81 us
    pallas_call x2, Pallas kernels, pack(): pl.pallas_call(functools.partial(pack_kernel, count, kinds, head_cols, fi...  4.76 us
    pallas_call x1, Pallas kernels, refine(): pl.pallas_call(edge_kernel, out_shape=jax.ShapeDtypeStruct((1, rows, chan...  4.39 us
    pallas_call x1, Pallas kernels, refine(): pl.pallas_call(inner_kernel, out_shape=jax.ShapeDtypeStruct((rows, channe...  4.16 us
  transfers between devices with their start and end apart: 31, of which 5 were waited for; matrix products, arithmetic and copies ran while one was open for 5% of the time, Pallas kernels for 18%

profile of v1, /device:TPU:1, one launch (start us, length us, event | category | flops | bytes accessed | tf_op | source)
XLA Modules:
  0.0 152.9 jit_solution(6600510383695722234)
XLA Ops:
  0.0 2.7 %pack.2 = (bf16[3,128,384]{2,1,0:T(8,128)(2,1)}, bf16[3,128,384]{2,1,0:T(8,128)(2,1)}, bf16[3,128,384]{2,1,0:T(8,128)(2,1)}, bf16[3,128,384]{2,1,0:T(8,128)(2,1)...) custom-call(bf16[1,128,4096]{2,1,0:T(8,128)(2,1)} %rest_0_.3, ...), custom_call_target="tpu_custom_call" | custom-call | bytes 4718592 | tf_op jit(solution)/shard_map/pack/pallas_call | solution.py:72
  2.8 2.8 %collective-permute-start.16 = (bf16[3,128,384]{2,1,0:T(8,128)(2,1)}, bf16[3,128,384]{2,1,0:T(8,128)(2,1)}, u32[]{:S(2)}, u32[]{:S(2)}) collective-permute-start(bf16[3,128,384]{2,1,0:T(8,128)(2,1)} %get-tuple-element.76), channel_id=1, source_target_pairs={{0,2},{1,3},{2,0},{3,1},{4,6},{5,7},{6,4},{7,5},{8,10},{9,11},{10,... | collective-permute-start | bytes 884744 | tf_op jit(solution)/shard_map/ppermute | solution.py:39
  5.6 2.0 %pack.3 = (bf16[3,128,128]{2,1,0:T(8,128)(2,1)}, bf16[3,128,128]{2,1,0:T(8,128)(2,1)}, bf16[3,128,128]{2,1,0:T(8,128)(2,1)}, bf16[3,128,128]{2,1,0:T(8,128)(2,1)...) custom-call(bf16[1,128,4096]{2,1,0:T(8,128)(2,1)} %rest_0_.3, ...), custom_call_target="tpu_custom_call" | custom-call | bytes 1572864 | tf_op jit(solution)/shard_map/pack/pallas_call | solution.py:72
  8.1 1.8 %collective-permute-start.17 = (bf16[3,128,384]{2,1,0:T(8,128)(2,1)}, bf16[3,128,384]{2,1,0:T(8,128)(2,1)}, u32[]{:S(2)}, u32[]{:S(2)}) collective-permute-start(bf16[3,128,384]{2,1,0:T(8,128)(2,1)} %get-tuple-element.77), channel_id=1, source_target_pairs={{0,3},{1,2},{2,1},{3,0},{4,7},{5,6},{6,5},{7,4},{8,11},{9,10},{10,... | collective-permute-start | bytes 884744 | tf_op jit(solution)/shard_map/ppermute | solution.py:39
  9.8 2.3 %collective-permute-start.18 = (bf16[3,128,384]{2,1,0:T(8,128)(2,1)}, bf16[3,128,384]{2,1,0:T(8,128)(2,1)}, u32[]{:S(2)}, u32[]{:S(2)}) collective-permute-start(bf16[3,128,384]{2,1,0:T(8,128)(2,1)} %get-tuple-element.78), channel_id=1, source_target_pairs={{0,4},{1,5},{2,6},{3,7},{4,0},{5,1},{6,2},{7,3},{8,12},{9,13},{10,... | collective-permute-start | bytes 884744 | tf_op jit(solution)/shard_map/ppermute | solution.py:39
  12.2 9.5 %collective-permute-done.30.rest_2_ = bf16[3,128,128]{2,1,0:T(8,128)(2,1)} collective-permute-done((bf16[3,128,128]{2,1,0:T(8,128)(2,1)}, bf16[3,128,128]{2,1,0:T(8,128)(2,1)}, u32[]{:S(2)}, u32[]{:S(2)}) %collective-permute-start.30) | collective-permute-done | bytes 98336 | tf_op jit(solution)/shard_map/ppermute | solution.py:39
  21.6 2.7 %collective-permute-start.19 = (bf16[3,128,384]{2,1,0:T(8,128)(2,1)}, bf16[3,128,384]{2,1,0:T(8,128)(2,1)}, u32[]{:S(2)}, u32[]{:S(2)}) collective-permute-start(bf16[3,128,384]{2,1,0:T(8,128)(2,1)} %get-tuple-element.79), channel_id=1, source_target_pairs={{0,5},{1,4},{2,7},{3,6},{4,1},{5,0},{6,3},{7,2},{8,13},{9,12},{10,... | collective-permute-start | bytes 884744 | tf_op jit(solution)/shard_map/ppermute | solution.py:39
  24.9 1.9 %collective-permute-start.21 = (bf16[3,128,384]{2,1,0:T(8,128)(2,1)}, bf16[3,128,384]{2,1,0:T(8,128)(2,1)}, u32[]{:S(2)}, u32[]{:S(2)}) collective-permute-start(bf16[3,128,384]{2,1,0:T(8,128)(2,1)} %get-tuple-element.81), channel_id=1, source_target_pairs={{0,7},{1,6},{2,5},{3,4},{4,3},{5,2},{6,1},{7,0},{8,15},{9,14},{10,... | collective-permute-start | bytes 884744 | tf_op jit(solution)/shard_map/ppermute | solution.py:39
  31.5 1.5 collective-permute-start.31
  33.4 24.4 %collective-permute-done.19.rest_5_ = bf16[3,128,384]{2,1,0:T(8,128)(2,1)} collective-permute-done((bf16[3,128,384]{2,1,0:T(8,128)(2,1)}, bf16[3,128,384]{2,1,0:T(8,128)(2,1)}, u32[]{:S(2)}, u32[]{:S(2)}) %collective-permute-start.19) | collective-permute-done | bytes 294944 | tf_op jit(solution)/shard_map/ppermute | solution.py:39
  58.8 2.8 %collective-permute-start.35 = (bf16[3,128,128]{2,1,0:T(8,128)(2,1)}, bf16[3,128,128]{2,1,0:T(8,128)(2,1)}, u32[]{:S(2)}, u32[]{:S(2)}) collective-permute-start(bf16[3,128,128]{2,1,0:T(8,128)(2,1)} %get-tuple-element.103), channel_id=1, source_target_pairs={{0,7},{1,6},{2,5},{3,4},{4,3},{5,2},{6,1},{7,0},{8,15},{9,14},{10,... | collective-permute-start | bytes 294920 | tf_op jit(solution)/shard_map/ppermute | solution.py:39
  61.7 7.9 %attend.2 = (bf16[128,384]{1,0:T(8,128)(2,1)}, bf16[128,384]{1,0:T(8,128)(2,1)}, bf16[128,384]{1,0:T(8,128)(2,1)}, bf16[128,384]{1,0:T(8,128)(2,1)}, bf16[128,38...) custom-call(s32[1]{0:T(128)} %get-tuple-element.116.frames_ref, ...), custom_call_target="tpu_custom_call" | custom-call | flops 2415919104 | bytes 3145728 | tf_op jit(solution)/shard_map/attend/pallas_call | solution.py:165
  69.7 9.2 %collective-permute-done.32.rest_4_ = bf16[3,128,128]{2,1,0:T(8,128)(2,1)} collective-permute-done((bf16[3,128,128]{2,1,0:T(8,128)(2,1)}, bf16[3,128,128]{2,1,0:T(8,128)(2,1)}, u32[]{:S(2)}, u32[]{:S(2)}) %collective-permute-start.32) | collective-permute-done | bytes 98336 | tf_op jit(solution)/shard_map/ppermute | solution.py:39
  78.9 6.8 %collective-permute-start.23 = (bf16[128,384]{1,0:T(8,128)(2,1)}, bf16[128,384]{1,0:T(8,128)(2,1)}, u32[]{:S(2)}, u32[]{:S(2)}) collective-permute-start(bf16[128,384]{1,0:T(8,128)(2,1)} %get-tuple-element.84), channel_id=1, source_target_pairs={{0,2},{1,3},{2,0},{3,1},{4,6},{5,7},{6,4},{7,5},{8,10},{9,11},{10,... | collective-permute-start | bytes 294920 | tf_op jit(solution)/shard_map/ppermute | solution.py:39
  85.7 4.4 %attend.3 = (bf16[128,128]{1,0:T(8,128)(2,1)}, bf16[128,128]{1,0:T(8,128)(2,1)}, bf16[128,128]{1,0:T(8,128)(2,1)}, bf16[128,128]{1,0:T(8,128)(2,1)}, bf16[128,12...) custom-call(s32[1]{0:T(128)} %get-tuple-element.116.frames_ref, ...), custom_call_target="tpu_custom_call" | custom-call | flops 805306368 | bytes 1048576 | tf_op jit(solution)/shard_map/attend/pallas_call | solution.py:165
  94.3 1.8 %collective-permute-start.24 = (bf16[128,384]{1,0:T(8,128)(2,1)}, bf16[128,384]{1,0:T(8,128)(2,1)}, u32[]{:S(2)}, u32[]{:S(2)}) collective-permute-start(bf16[128,384]{1,0:T(8,128)(2,1)} %get-tuple-element.85), channel_id=1, source_target_pairs={{0,3},{1,2},{2,1},{3,0},{4,7},{5,6},{6,5},{7,4},{8,11},{9,10},{10,... | collective-permute-start | bytes 294920 | tf_op jit(solution)/shard_map/ppermute | solution.py:39
  96.9 1.9 %collective-permute-start.26 = (bf16[128,384]{1,0:T(8,128)(2,1)}, bf16[128,384]{1,0:T(8,128)(2,1)}, u32[]{:S(2)}, u32[]{:S(2)}) collective-permute-start(bf16[128,384]{1,0:T(8,128)(2,1)} %get-tuple-element.87), channel_id=1, source_target_pairs={{0,5},{1,4},{2,7},{3,6},{4,1},{5,0},{6,3},{7,2},{8,13},{9,12},{10,... | collective-permute-start | bytes 294920 | tf_op jit(solution)/shard_map/ppermute | solution.py:39
  98.8 2.1 %collective-permute-start.27 = (bf16[128,384]{1,0:T(8,128)(2,1)}, bf16[128,384]{1,0:T(8,128)(2,1)}, u32[]{:S(2)}, u32[]{:S(2)}) collective-permute-start(bf16[128,384]{1,0:T(8,128)(2,1)} %get-tuple-element.88), channel_id=1, source_target_pairs={{0,6},{1,7},{2,4},{3,5},{4,2},{5,3},{6,0},{7,1},{8,14},{9,15},{10,... | collective-permute-start | bytes 294920 | tf_op jit(solution)/shard_map/ppermute | solution.py:39
  103.5 2.4 %collective-permute-start.39 = (bf16[128,128]{1,0:T(8,128)(2,1)}, bf16[128,128]{1,0:T(8,128)(2,1)}, u32[]{:S(2)}, u32[]{:S(2)}) collective-permute-start(bf16[128,128]{1,0:T(8,128)(2,1)} %get-tuple-element.108), channel_id=1, source_target_pairs={{0,4},{1,5},{2,6},{3,7},{4,0},{5,1},{6,2},{7,3},{8,12},{9,13},{10,... | collective-permute-start | bytes 98312 | tf_op jit(solution)/shard_map/ppermute | solution.py:39
  105.9 7.1 %collective-permute-done.26.rest_5_ = bf16[128,384]{1,0:T(8,128)(2,1)} collective-permute-done((bf16[128,384]{1,0:T(8,128)(2,1)}, bf16[128,384]{1,0:T(8,128)(2,1)}, u32[]{:S(2)}, u32[]{:S(2)}) %collective-permute-start.26) | collective-permute-done | bytes 98336 | tf_op jit(solution)/shard_map/ppermute | solution.py:39
  114.2 2.4 %collective-permute-start.41 = (bf16[128,128]{1,0:T(8,128)(2,1)}, bf16[128,128]{1,0:T(8,128)(2,1)}, u32[]{:S(2)}, u32[]{:S(2)}) collective-permute-start(bf16[128,128]{1,0:T(8,128)(2,1)} %get-tuple-element.110), channel_id=1, source_target_pairs={{0,6},{1,7},{2,4},{3,5},{4,2},{5,3},{6,0},{7,1},{8,14},{9,15},{10,... | collective-permute-start | bytes 98312 | tf_op jit(solution)/shard_map/ppermute | solution.py:39
  116.6 2.1 %fusion.1 = s32[]{:T(128)} fusion(s32[15]{0:T(128)} %constant.34.clone, s32[]{:T(128)} %get-tuple-element.112), kind=kLoop, calls=%fused_computation.7 | loop fusion | flops 44 | bytes 68 | tf_op jit(solution)/shard_map/reduce_sum | solution.py:626
  120.0 2.9 %constants.1.rest_6_ = f32[2,8,256]{2,1,0:T(8,128)} custom-call(f32[3,4096]{1,0:T(4,128)} %bitcast.7, bf16[4096,256]{1,0:T(8,128)(2,1)} %weight_ref.3), custom_call_target="tpu_custom_call" | custom-call | flops 67108864 | bytes 2097152 | tf_op jit(solution)/shard_map/constants/pallas_call | solution.py:286
  122.9 6.1 %project_early.1 = (f32[128,256]{1,0:T(8,128)}, f32[128,128]{1,0:T(8,128)}, f32[128,128]{1,0:T(8,128)}, bf16[128,1024]{1,0:T(8,128)(2,1)}, f32[3,1024]{1,0:T(4,128)}, /*index=5*/bf16[1024,256]{1,0:T(8,128)(2,1)}) custom-call(bf16[1,128,4096]{2,1,0:T(8,128)(2,1)} %h_ref.1, f32[3,4096]{1,0:T(4,128)} %bitcast.8, bf16[4096,256]{1,0:T(8,128)(2,1)} %weight_ref.3, ...), custom_call_target="tpu_custom_call" | custom-call | flops 201326592 | bytes 4194304 | tf_op jit(solution)/shard_map/project_early/pallas_call | solution.py:384
  129.0 3.1 %project_late.1 = bf16[128,256]{1,0:T(8,128)(2,1)} custom-call(s32[1]{0:T(128)} %get-tuple-element.116.frames_ref, f32[128,256]{1,0:T(8,128)} %get-tuple-element.90.rest_0_, f32[128,128]{1,0:T(8,128)} %get-tuple-element.91.rest_1_, f32[128,128]{1,0:T(8,128)} %get-tuple-element.92.rest_2_, bf16[128,1024]{1,0:T(8,128)(2,1)} %get-tuple-element.93.rest_3_, ...), custom_call_target="tpu_custom_call" | custom-call | flops 67108864 | bytes 524288 | tf_op jit(solution)/shard_map/project_late/pallas_call | solution.py:467
  132.1 3.9 %conditional.1 = (bf16[128,256]{1,0:T(8,128)(2,1)}) conditional(s32[]{:T(128)} %clamp.3, bf16[128,256]{1,0:T(8,128)(2,1)} %project_late.1, bf16[128,256]{1,0:T(8,128)(2,1)} %project_late.1, bf16[128,256]{1,0:T(8,128)(2,1)} %project_late.1, bf16[128,256]{1,0:T(8,128)(2,1)} %project_late.1, ...), branch_computations={%region_3.4_spmd, %region_4.5_spmd, %region_5.6_spmd, %region_6.7_... | conditional | bytes 262192 | solution.py:627
  132.2 2.2 %collective-permute-start.14 = (bf16[128,256]{1,0:T(8,128)(2,1)}, bf16[128,256]{1,0:T(8,128)(2,1)}, u32[]{:S(2)}, u32[]{:S(2)}) collective-permute-start(bf16[128,256]{1,0:T(8,128)(2,1)} %param.14), channel_id=1, source_target_pairs={{0,24},{8,16},{16,0},{24,8},{1,25},{9,17},{17,1},{25,9},{2,26},{10... | collective-permute-start | bytes 196616 | tf_op jit(solution)/shard_map/cond/branch_14_fun/ppermute | solution.py:620
  134.4 1.6 %collective-permute-done.14 = bf16[128,256]{1,0:T(8,128)(2,1)} collective-permute-done((bf16[128,256]{1,0:T(8,128)(2,1)}, bf16[128,256]{1,0:T(8,128)(2,1)}, u32[]{:S(2)}, u32[]{:S(2)}) %collective-permute-start.14) | collective-permute-done | bytes 65568 | tf_op jit(solution)/shard_map/cond/branch_14_fun/ppermute | solution.py:620
  137.4 2.1 %collective-permute-start.43 = (bf16[64,256]{1,0:T(8,128)(2,1)}, bf16[64,256]{1,0:T(8,128)(2,1)}, u32[]{:S(2)}, u32[]{:S(2)}) collective-permute-start(bf16[64,256]{1,0:T(8,128)(2,1)} %get-tuple-element.115), channel_id=1, source_target_pairs={{0,1},{1,0},{2,3},{3,2},{4,5},{5,4},{6,7},{7,6},{8,9},{9,8},{10,11... | collective-permute-start | bytes 98312 | tf_op jit(solution)/shard_map/ppermute | solution.py:647
  139.5 4.8 %collective-permute-start.44 = (bf16[64,256]{1,0:T(8,128)(2,1)}, bf16[64,256]{1,0:T(8,128)(2,1)}, u32[]{:S(2)}, u32[]{:S(2)}) collective-permute-start(bf16[64,256]{1,0:T(8,128)(2,1)} %get-tuple-element.114), channel_id=1, source_target_pairs={{1,2},{3,4},{5,6},{2,1},{4,3},{6,5},{9,10},{11,12},{13,14},{10,9},... | collective-permute-start | bytes 98312 | tf_op jit(solution)/shard_map/ppermute | solution.py:647
  144.4 4.2 %refine_inner.1.inner_ref = f32[128,256]{1,0:T(8,128)} custom-call(bf16[128,256]{1,0:T(8,128)(2,1)} %get-tuple-element.118.mid_ref, bf16[3,2304,256]{2,1,0:T(8,128)(2,1)} %bitcast.5), custom_call_target="tpu_custom_call" | custom-call | flops 301989888 | bytes 3735552 | tf_op jit(solution)/shard_map/refine_inner/pallas_call | solution.py:573
  148.5 4.4 %refine_edge.1 = bf16[1,128,256]{2,1,0:T(8,128)(2,1)} custom-call(s32[1]{0:T(128)} %get-tuple-element.117.frames_ref, f32[128,256]{1,0:T(8,128)} %refine_inner.1.inner_ref, bf16[64,256]{1,0:T(8,128)(2,1)} %collective-permute-done.43.even_ref, bf16[64,256]{1,0:T(8,128)(2,1)} %collective-permute-done.44.odd_ref, bf16[3,2304,256]{2,1,0:T(8,128)(2,1)} %bitcast.6), custom_call_target="tpu_custom_call" | custom-call | flops 150994944 | bytes 3735552 | tf_op jit(solution)/shard_map/refine_edge/pallas_call | solution.py:591
  (51 shorter events, 14.1 us)
Async XLA Ops:
  2.7 21.6 %collective-permute-start.15 = (bf16[3,128,384]{2,1,0:T(8,128)(2,1)}, bf16[3,128,384]{2,1,0:T(8,128)(2,1)}, u32[]{:S(2)}, u32[]{:S(2)}) collective-permute-start(bf16[3,128,384]{2,1,0:T(8,128)(2,1)} %get-tuple-element.75), channel_id=1, source_target_pairs={{0,1},{1,0},{2,3},{3,2},{4,5},{5,4},{6,7},{7,6},{8,9},{9,8},{10,11... | collective-permute-start | bytes 884744 | tf_op jit(solution)/shard_map/ppermute | solution.py:39
  2.8 22.0 %collective-permute-start.16 = (bf16[3,128,384]{2,1,0:T(8,128)(2,1)}, bf16[3,128,384]{2,1,0:T(8,128)(2,1)}, u32[]{:S(2)}, u32[]{:S(2)}) collective-permute-start(bf16[3,128,384]{2,1,0:T(8,128)(2,1)} %get-tuple-element.76), channel_id=1, source_target_pairs={{0,2},{1,3},{2,0},{3,1},{4,6},{5,7},{6,4},{7,5},{8,10},{9,11},{10,... | collective-permute-start | bytes 884744 | tf_op jit(solution)/shard_map/ppermute | solution.py:39
  7.6 2.2 %collective-permute-start.29 = (bf16[3,128,128]{2,1,0:T(8,128)(2,1)}, bf16[3,128,128]{2,1,0:T(8,128)(2,1)}, u32[]{:S(2)}, u32[]{:S(2)}) collective-permute-start(bf16[3,128,128]{2,1,0:T(8,128)(2,1)} %get-tuple-element.97), channel_id=1, source_target_pairs={{0,1},{1,0},{2,3},{3,2},{4,5},{5,4},{6,7},{7,6},{8,9},{9,8},{10,11... | collective-permute-start | bytes 294920 | tf_op jit(solution)/shard_map/ppermute | solution.py:39
  8.1 13.6 %collective-permute-start.30 = (bf16[3,128,128]{2,1,0:T(8,128)(2,1)}, bf16[3,128,128]{2,1,0:T(8,128)(2,1)}, u32[]{:S(2)}, u32[]{:S(2)}) collective-permute-start(bf16[3,128,128]{2,1,0:T(8,128)(2,1)} %get-tuple-element.98), channel_id=1, source_target_pairs={{0,2},{1,3},{2,0},{3,1},{4,6},{5,7},{6,4},{7,5},{8,10},{9,11},{10,... | collective-permute-start | bytes 294920 | tf_op jit(solution)/shard_map/ppermute | solution.py:39
  8.1 23.4 %collective-permute-start.17 = (bf16[3,128,384]{2,1,0:T(8,128)(2,1)}, bf16[3,128,384]{2,1,0:T(8,128)(2,1)}, u32[]{:S(2)}, u32[]{:S(2)}) collective-permute-start(bf16[3,128,384]{2,1,0:T(8,128)(2,1)} %get-tuple-element.77), channel_id=1, source_target_pairs={{0,3},{1,2},{2,1},{3,0},{4,7},{5,6},{6,5},{7,4},{8,11},{9,10},{10,... | collective-permute-start | bytes 884744 | tf_op jit(solution)/shard_map/ppermute | solution.py:39
  9.8 23.1 %collective-permute-start.18 = (bf16[3,128,384]{2,1,0:T(8,128)(2,1)}, bf16[3,128,384]{2,1,0:T(8,128)(2,1)}, u32[]{:S(2)}, u32[]{:S(2)}) collective-permute-start(bf16[3,128,384]{2,1,0:T(8,128)(2,1)} %get-tuple-element.78), channel_id=1, source_target_pairs={{0,4},{1,5},{2,6},{3,7},{4,0},{5,1},{6,2},{7,3},{8,12},{9,13},{10,... | collective-permute-start | bytes 884744 | tf_op jit(solution)/shard_map/ppermute | solution.py:39
  21.6 36.2 %collective-permute-start.19 = (bf16[3,128,384]{2,1,0:T(8,128)(2,1)}, bf16[3,128,384]{2,1,0:T(8,128)(2,1)}, u32[]{:S(2)}, u32[]{:S(2)}) collective-permute-start(bf16[3,128,384]{2,1,0:T(8,128)(2,1)} %get-tuple-element.79), channel_id=1, source_target_pairs={{0,5},{1,4},{2,7},{3,6},{4,1},{5,0},{6,3},{7,2},{8,13},{9,12},{10,... | collective-permute-start | bytes 884744 | tf_op jit(solution)/shard_map/ppermute | solution.py:39
  24.3 33.5 %collective-permute-start.20 = (bf16[3,128,384]{2,1,0:T(8,128)(2,1)}, bf16[3,128,384]{2,1,0:T(8,128)(2,1)}, u32[]{:S(2)}, u32[]{:S(2)}) collective-permute-start(bf16[3,128,384]{2,1,0:T(8,128)(2,1)} %get-tuple-element.80), channel_id=1, source_target_pairs={{0,6},{1,7},{2,4},{3,5},{4,2},{5,3},{6,0},{7,1},{8,14},{9,15},{10,... | collective-permute-start | bytes 884744 | tf_op jit(solution)/shard_map/ppermute | solution.py:39
  24.9 34.0 %collective-permute-start.21 = (bf16[3,128,384]{2,1,0:T(8,128)(2,1)}, bf16[3,128,384]{2,1,0:T(8,128)(2,1)}, u32[]{:S(2)}, u32[]{:S(2)}) collective-permute-start(bf16[3,128,384]{2,1,0:T(8,128)(2,1)} %get-tuple-element.81), channel_id=1, source_target_pairs={{0,7},{1,6},{2,5},{3,4},{4,3},{5,2},{6,1},{7,0},{8,15},{9,14},{10,... | collective-permute-start | bytes 884744 | tf_op jit(solution)/shard_map/ppermute | solution.py:39
  31.5 38.1 %collective-permute-start.31 = (bf16[3,128,128]{2,1,0:T(8,128)(2,1)}, bf16[3,128,128]{2,1,0:T(8,128)(2,1)}, u32[]{:S(2)}, u32[]{:S(2)}) collective-permute-start(bf16[3,128,128]{2,1,0:T(8,128)(2,1)} %get-tuple-element.99), channel_id=1, source_target_pairs={{0,3},{1,2},{2,1},{3,0},{4,7},{5,6},{6,5},{7,4},{8,11},{9,10},{10,... | collective-permute-start | bytes 294920 | tf_op jit(solution)/shard_map/ppermute | solution.py:39
  33.0 45.9 %collective-permute-start.32 = (bf16[3,128,128]{2,1,0:T(8,128)(2,1)}, bf16[3,128,128]{2,1,0:T(8,128)(2,1)}, u32[]{:S(2)}, u32[]{:S(2)}) collective-permute-start(bf16[3,128,128]{2,1,0:T(8,128)(2,1)} %get-tuple-element.100), channel_id=1, source_target_pairs={{0,4},{1,5},{2,6},{3,7},{4,0},{5,1},{6,2},{7,3},{8,12},{9,13},{10,... | collective-permute-start | bytes 294920 | tf_op jit(solution)/shard_map/ppermute | solution.py:39
  57.8 27.8 %collective-permute-start.33 = (bf16[3,128,128]{2,1,0:T(8,128)(2,1)}, bf16[3,128,128]{2,1,0:T(8,128)(2,1)}, u32[]{:S(2)}, u32[]{:S(2)}) collective-permute-start(bf16[3,128,128]{2,1,0:T(8,128)(2,1)} %get-tuple-element.101), channel_id=1, source_target_pairs={{0,5},{1,4},{2,7},{3,6},{4,1},{5,0},{6,3},{7,2},{8,13},{9,12},{10,... | collective-permute-start | bytes 294920 | tf_op jit(solution)/shard_map/ppermute | solution.py:39
  57.8 27.8 %collective-permute-start.34 = (bf16[3,128,128]{2,1,0:T(8,128)(2,1)}, bf16[3,128,128]{2,1,0:T(8,128)(2,1)}, u32[]{:S(2)}, u32[]{:S(2)}) collective-permute-start(bf16[3,128,128]{2,1,0:T(8,128)(2,1)} %get-tuple-element.102), channel_id=1, source_target_pairs={{0,6},{1,7},{2,4},{3,5},{4,2},{5,3},{6,0},{7,1},{8,14},{9,15},{10,... | collective-permute-start | bytes 294920 | tf_op jit(solution)/shard_map/ppermute | solution.py:39
  58.8 26.8 %collective-permute-start.35 = (bf16[3,128,128]{2,1,0:T(8,128)(2,1)}, bf16[3,128,128]{2,1,0:T(8,128)(2,1)}, u32[]{:S(2)}, u32[]{:S(2)}) collective-permute-start(bf16[3,128,128]{2,1,0:T(8,128)(2,1)} %get-tuple-element.103), channel_id=1, source_target_pairs={{0,7},{1,6},{2,5},{3,4},{4,3},{5,2},{6,1},{7,0},{8,15},{9,14},{10,... | collective-permute-start | bytes 294920 | tf_op jit(solution)/shard_map/ppermute | solution.py:39
  69.6 29.2 %collective-permute-start.22 = (bf16[128,384]{1,0:T(8,128)(2,1)}, bf16[128,384]{1,0:T(8,128)(2,1)}, u32[]{:S(2)}, u32[]{:S(2)}) collective-permute-start(bf16[128,384]{1,0:T(8,128)(2,1)} %get-tuple-element.83), channel_id=1, source_target_pairs={{0,1},{1,0},{2,3},{3,2},{4,5},{5,4},{6,7},{7,6},{8,9},{9,8},{10,11... | collective-permute-start | bytes 294920 | tf_op jit(solution)/shard_map/ppermute | solution.py:39
  78.9 22.0 %collective-permute-start.23 = (bf16[128,384]{1,0:T(8,128)(2,1)}, bf16[128,384]{1,0:T(8,128)(2,1)}, u32[]{:S(2)}, u32[]{:S(2)}) collective-permute-start(bf16[128,384]{1,0:T(8,128)(2,1)} %get-tuple-element.84), channel_id=1, source_target_pairs={{0,2},{1,3},{2,0},{3,1},{4,6},{5,7},{6,4},{7,5},{8,10},{9,11},{10,... | collective-permute-start | bytes 294920 | tf_op jit(solution)/shard_map/ppermute | solution.py:39
  90.1 5.9 %collective-permute-start.36 = (bf16[128,128]{1,0:T(8,128)(2,1)}, bf16[128,128]{1,0:T(8,128)(2,1)S(1)}, u32[]{:S(2)}, u32[]{:S(2)}) collective-permute-start(bf16[128,128]{1,0:T(8,128)(2,1)} %get-tuple-element.105), channel_id=1, source_target_pairs={{0,1},{1,0},{2,3},{3,2},{4,5},{5,4},{6,7},{7,6},{8,9},{9,8},{10,11... | collective-permute-start | bytes 98312 | tf_op jit(solution)/shard_map/ppermute | solution.py:39
  90.9 6.0 %collective-permute-start.37 = (bf16[128,128]{1,0:T(8,128)(2,1)}, bf16[128,128]{1,0:T(8,128)(2,1)S(1)}, u32[]{:S(2)}, u32[]{:S(2)}) collective-permute-start(bf16[128,128]{1,0:T(8,128)(2,1)} %get-tuple-element.106), channel_id=1, source_target_pairs={{0,2},{1,3},{2,0},{3,1},{4,6},{5,7},{6,4},{7,5},{8,10},{9,11},{10,... | collective-permute-start | bytes 98312 | tf_op jit(solution)/shard_map/ppermute | solution.py:39
  94.3 9.1 %collective-permute-start.24 = (bf16[128,384]{1,0:T(8,128)(2,1)}, bf16[128,384]{1,0:T(8,128)(2,1)}, u32[]{:S(2)}, u32[]{:S(2)}) collective-permute-start(bf16[128,384]{1,0:T(8,128)(2,1)} %get-tuple-element.85), channel_id=1, source_target_pairs={{0,3},{1,2},{2,1},{3,0},{4,7},{5,6},{6,5},{7,4},{8,11},{9,10},{10,... | collective-permute-start | bytes 294920 | tf_op jit(solution)/shard_map/ppermute | solution.py:39
  96.1 4.8 %copy-start = (bf16[128,128]{1,0:T(8,128)(2,1)}, bf16[128,128]{1,0:T(8,128)(2,1)S(1)}, u32[]{:S(2)}) copy-start(bf16[128,128]{1,0:T(8,128)(2,1)S(1)} %collective-permute-done.36.rest_8_) | copy-start | bytes 98308
  96.1 7.4 %collective-permute-start.25 = (bf16[128,384]{1,0:T(8,128)(2,1)}, bf16[128,384]{1,0:T(8,128)(2,1)}, u32[]{:S(2)}, u32[]{:S(2)}) collective-permute-start(bf16[128,384]{1,0:T(8,128)(2,1)} %get-tuple-element.86), channel_id=1, source_target_pairs={{0,4},{1,5},{2,6},{3,7},{4,0},{5,1},{6,2},{7,3},{8,12},{9,13},{10,... | collective-permute-start | bytes 294920 | tf_op jit(solution)/shard_map/ppermute | solution.py:39
  96.9 16.1 %collective-permute-start.26 = (bf16[128,384]{1,0:T(8,128)(2,1)}, bf16[128,384]{1,0:T(8,128)(2,1)}, u32[]{:S(2)}, u32[]{:S(2)}) collective-permute-start(bf16[128,384]{1,0:T(8,128)(2,1)} %get-tuple-element.87), channel_id=1, source_target_pairs={{0,5},{1,4},{2,7},{3,6},{4,1},{5,0},{6,3},{7,2},{8,13},{9,12},{10,... | collective-permute-start | bytes 294920 | tf_op jit(solution)/shard_map/ppermute | solution.py:39
  98.8 15.4 %collective-permute-start.27 = (bf16[128,384]{1,0:T(8,128)(2,1)}, bf16[128,384]{1,0:T(8,128)(2,1)}, u32[]{:S(2)}, u32[]{:S(2)}) collective-permute-start(bf16[128,384]{1,0:T(8,128)(2,1)} %get-tuple-element.88), channel_id=1, source_target_pairs={{0,6},{1,7},{2,4},{3,5},{4,2},{5,3},{6,0},{7,1},{8,14},{9,15},{10,... | collective-permute-start | bytes 294920 | tf_op jit(solution)/shard_map/ppermute | solution.py:39
  100.9 15.7 %collective-permute-start.28 = (bf16[128,384]{1,0:T(8,128)(2,1)}, bf16[128,384]{1,0:T(8,128)(2,1)}, u32[]{:S(2)}, u32[]{:S(2)}) collective-permute-start(bf16[128,384]{1,0:T(8,128)(2,1)} %get-tuple-element.89), channel_id=1, source_target_pairs={{0,7},{1,6},{2,5},{3,4},{4,3},{5,2},{6,1},{7,0},{8,15},{9,14},{10,... | collective-permute-start | bytes 294920 | tf_op jit(solution)/shard_map/ppermute | solution.py:39
  103.4 25.6 %collective-permute-start.38 = (bf16[128,128]{1,0:T(8,128)(2,1)}, bf16[128,128]{1,0:T(8,128)(2,1)}, u32[]{:S(2)}, u32[]{:S(2)}) collective-permute-start(bf16[128,128]{1,0:T(8,128)(2,1)} %get-tuple-element.107), channel_id=1, source_target_pairs={{0,3},{1,2},{2,1},{3,0},{4,7},{5,6},{6,5},{7,4},{8,11},{9,10},{10,... | collective-permute-start | bytes 98312 | tf_op jit(solution)/shard_map/ppermute | solution.py:39
  103.5 25.5 %collective-permute-start.39 = (bf16[128,128]{1,0:T(8,128)(2,1)}, bf16[128,128]{1,0:T(8,128)(2,1)}, u32[]{:S(2)}, u32[]{:S(2)}) collective-permute-start(bf16[128,128]{1,0:T(8,128)(2,1)} %get-tuple-element.108), channel_id=1, source_target_pairs={{0,4},{1,5},{2,6},{3,7},{4,0},{5,1},{6,2},{7,3},{8,12},{9,13},{10,... | collective-permute-start | bytes 98312 | tf_op jit(solution)/shard_map/ppermute | solution.py:39
  113.0 16.0 %collective-permute-start.40 = (bf16[128,128]{1,0:T(8,128)(2,1)}, bf16[128,128]{1,0:T(8,128)(2,1)}, u32[]{:S(2)}, u32[]{:S(2)}) collective-permute-start(bf16[128,128]{1,0:T(8,128)(2,1)} %get-tuple-element.109), channel_id=1, source_target_pairs={{0,5},{1,4},{2,7},{3,6},{4,1},{5,0},{6,3},{7,2},{8,13},{9,12},{10,... | collective-permute-start | bytes 98312 | tf_op jit(solution)/shard_map/ppermute | solution.py:39
  114.2 14.8 %collective-permute-start.41 = (bf16[128,128]{1,0:T(8,128)(2,1)}, bf16[128,128]{1,0:T(8,128)(2,1)}, u32[]{:S(2)}, u32[]{:S(2)}) collective-permute-start(bf16[128,128]{1,0:T(8,128)(2,1)} %get-tuple-element.110), channel_id=1, source_target_pairs={{0,6},{1,7},{2,4},{3,5},{4,2},{5,3},{6,0},{7,1},{8,14},{9,15},{10,... | collective-permute-start | bytes 98312 | tf_op jit(solution)/shard_map/ppermute | solution.py:39
  116.6 12.4 %collective-permute-start.42 = (bf16[128,128]{1,0:T(8,128)(2,1)}, bf16[128,128]{1,0:T(8,128)(2,1)}, u32[]{:S(2)}, u32[]{:S(2)}) collective-permute-start(bf16[128,128]{1,0:T(8,128)(2,1)} %get-tuple-element.111), channel_id=1, source_target_pairs={{0,7},{1,6},{2,5},{3,4},{4,3},{5,2},{6,1},{7,0},{8,15},{9,14},{10,... | collective-permute-start | bytes 98312 | tf_op jit(solution)/shard_map/ppermute | solution.py:39
  132.2 3.9 %collective-permute-start.14 = (bf16[128,256]{1,0:T(8,128)(2,1)}, bf16[128,256]{1,0:T(8,128)(2,1)}, u32[]{:S(2)}, u32[]{:S(2)}) collective-permute-start(bf16[128,256]{1,0:T(8,128)(2,1)} %param.14), channel_id=1, source_target_pairs={{0,24},{8,16},{16,0},{24,8},{1,25},{9,17},{17,1},{25,9},{2,26},{10... | collective-permute-start | bytes 196616 | tf_op jit(solution)/shard_map/cond/branch_14_fun/ppermute | solution.py:620
  137.4 11.1 %collective-permute-start.43 = (bf16[64,256]{1,0:T(8,128)(2,1)}, bf16[64,256]{1,0:T(8,128)(2,1)}, u32[]{:S(2)}, u32[]{:S(2)}) collective-permute-start(bf16[64,256]{1,0:T(8,128)(2,1)} %get-tuple-element.115), channel_id=1, source_target_pairs={{0,1},{1,0},{2,3},{3,2},{4,5},{5,4},{6,7},{7,6},{8,9},{9,8},{10,11... | collective-permute-start | bytes 98312 | tf_op jit(solution)/shard_map/ppermute | solution.py:647
  139.5 9.0 %collective-permute-start.44 = (bf16[64,256]{1,0:T(8,128)(2,1)}, bf16[64,256]{1,0:T(8,128)(2,1)}, u32[]{:S(2)}, u32[]{:S(2)}) collective-permute-start(bf16[64,256]{1,0:T(8,128)(2,1)} %get-tuple-element.114), channel_id=1, source_target_pairs={{1,2},{3,4},{5,6},{2,1},{4,3},{6,5},{9,10},{11,12},{13,14},{10,9},... | collective-permute-start | bytes 98312 | tf_op jit(solution)/shard_map/ppermute | solution.py:647
  (1 other events, 4.0 us)
